TPU v7x, 32 devices: a whole 2x2x4 slice. The times are simulated.
32 devices in a mesh: grp: 4 (over y, x), ext: 8 (over z, core).
Axes of the slice: x: 2, y: 2, z: 4, core: 2. Of those that a mesh axis runs over, the one named last changes fastest.
Arguments:
- tiles: bfloat16 [576, 49, 2048], P(('grp', 'ext')), may hold values from -6 to 6
- tissue_index: int32 [32, 18], P(('grp', 'ext')), may hold values from 0 to 17, each once within a row
- tissue_count: int32 [32], P(('grp', 'ext')), may hold values from 0 to 16, as said below
- w_reduce: bfloat16 [2048, 512], replicated, may hold values from -0.125 to 0.125
- scale_reduce: float32 [512], replicated, may hold values from 0.5 to 2
- bias_reduce: float32 [512], replicated, may hold values from -3 to 3
- w_spatial: bfloat16 [3, 3, 512, 512], replicated, may hold values from -0.09375 to 0.09375
- scale_spatial: float32 [512], replicated, may hold values from 0.5 to 2
- bias_spatial: float32 [512], replicated, may hold values from -3 to 3
- w_expand: bfloat16 [512, 2048], replicated, may hold values from -0.25 to 0.25
- scale_expand: float32 [2048], replicated, may hold values from 0.5 to 2
- bias_expand: float32 [2048], replicated, may hold values from -3 to 3
Outputs:
- embeddings: bfloat16 [256, 2048], P(('grp', 'ext'))
Inputs may be any that keep to these rules, and one draw needn't show every extreme that they name: Let S(d) be the sum of tissue_count over owners before owner d; then 8 * d <= S(d) <= 8 * (d + 1) for every d, and all counts sum to 256.
All inputs are finite; a program needn't handle non-finite values.
Results may differ from a plain program's by a relative error of at most 0.0021.
Values may be sent and summed in bfloat16 or wider, within the bound.
No kernel may reach another device: no remote copies, remote signals or barrier semaphores. Data moves between devices by JAX's collectives and lax.ppermute only.
A program may use at most 128 MiB of HBM per device.

v0:
```python
import jax
import jax.numpy as jnp
from jax import lax
from jax.sharding import PartitionSpec as P

SIDE = 7
SEQ_DEV = 8


def passed_along(x, axis, by):
    devices = lax.axis_size(axis)
    pairs = [(i, i + by) for i in range(devices) if 0 <= i + by < devices]
    return lax.ppermute(x, axis, pairs)


def bottleneck(
    tile_maps,
    w_reduce,
    scale_reduce,
    bias_reduce,
    w_spatial,
    scale_spatial,
    bias_spatial,
    w_expand,
    scale_expand,
    bias_expand,
):
    count_tiles = tile_maps.shape[0]
    side_cells = SIDE
    channels = tile_maps.shape[2]
    inner = w_reduce.shape[1]
    flat_map = tile_maps.reshape(count_tiles * side_cells * side_cells, channels)
    reduced = jnp.maximum(
        jnp.dot(flat_map, w_reduce, preferred_element_type=jnp.float32) * scale_reduce
        + bias_reduce,
        0.0,
    ).astype(jnp.bfloat16)
    grid_map = reduced.reshape(count_tiles, side_cells, side_cells, inner)
    padded = jnp.pad(grid_map, ((0, 0), (1, 1), (1, 1), (0, 0)))
    summed = jnp.zeros((count_tiles * side_cells * side_cells, inner), jnp.float32)
    for row_shift in range(3):
        for col_shift in range(3):
            window = padded[
                :, row_shift : row_shift + side_cells, col_shift : col_shift + side_cells, :
            ].reshape(count_tiles * side_cells * side_cells, inner)
            summed = summed + jnp.dot(
                window, w_spatial[row_shift, col_shift], preferred_element_type=jnp.float32
            )
    spatial = jnp.maximum(summed * scale_spatial + bias_spatial, 0.0).astype(jnp.bfloat16)
    expanded = jnp.maximum(
        jnp.dot(spatial, w_expand, preferred_element_type=jnp.float32) * scale_expand
        + bias_expand
        + flat_map.astype(jnp.float32),
        0.0,
    )
    return jnp.mean(
        expanded.reshape(count_tiles, side_cells * side_cells, channels), axis=1
    ).astype(jnp.bfloat16)


def on_device(
    tiles,
    tissue_index,
    tissue_count,
    w_reduce,
    scale_reduce,
    bias_reduce,
    w_spatial,
    scale_spatial,
    bias_spatial,
    w_expand,
    scale_expand,
    bias_expand,
):
    shard_rows = SEQ_DEV
    owned_count = tissue_count[0]
    rank_here = lax.axis_index(("grp", "ext"))
    every_count = lax.all_gather(tissue_count, ("grp", "ext"), axis=0, tiled=True)
    before = jnp.arange(every_count.shape[0], dtype=jnp.int32) < rank_here
    offset = jnp.sum(jnp.where(before, every_count, 0))
    backlog = offset - rank_here * shard_rows
    row_order = jnp.arange(shard_rows, dtype=jnp.int32)
    listing = tissue_index[0]
    last_slot = 2 * shard_rows - 1
    stay_slot = jnp.clip(row_order - backlog, 0, last_slot)
    spill_raw = shard_rows - backlog + row_order
    spill_live = spill_raw < owned_count
    spill_slot = jnp.clip(spill_raw, 0, last_slot)
    from_prior = row_order < backlog
    weights = (
        w_reduce,
        scale_reduce,
        bias_reduce,
        w_spatial,
        scale_spatial,
        bias_spatial,
        w_expand,
        scale_expand,
        bias_expand,
    )
    spill_maps = jnp.where(
        spill_live[:, None, None], tiles[listing[spill_slot]], jnp.zeros((), jnp.bfloat16)
    )
    arrived = passed_along(spill_maps, ("grp", "ext"), 1)
    own_tiles = tiles[listing[stay_slot]]
    shard_tiles = jnp.where(from_prior[:, None, None], arrived, own_tiles)
    return bottleneck(shard_tiles, *weights)


def solution(mesh):
    placed = (
        P(("grp", "ext"), None, None),
        P(("grp", "ext"), None),
        P(("grp", "ext")),
        P(),
        P(),
        P(),
        P(),
        P(),
        P(),
        P(),
        P(),
        P(),
    )
    return jax.shard_map(
        on_device, mesh=mesh, in_specs=placed, out_specs=P(("grp", "ext"), None), check_vma=False
    )
```

profile of v0, /device:TPU:4, one launch (start us, length us, event | category | flops | bytes accessed | tf_op | source)
XLA Modules:
  0.0 132.1 jit_solution(6737965803546858395)
XLA Ops:
  0.0 0.0 copy-start
  0.8 0.1 dynamic-update-slice
  0.9 41.2 %all-reduce.1 = s32[32]{0:T(128)S(1)} all-reduce(s32[32]{0:T(128)S(1)} %dynamic-update-slice), channel_id=1, replica_groups=mesh['grp'=4,'ext'=8] {'grp','ext'}, use_global_device_ids=true, to_apply=%add.1 | all-reduce | flops 32 | bytes 256
  42.2 0.7 fusion.31
  43.6 1.3 gather_fusion
  44.9 4.1 %gather_fusion.1 = bf16[8,49,2048]{2,1,0:T(8,128)(2,1)} fusion(bf16[18,49,2048]{2,1,0:T(8,128)(2,1)} %param.12, s32[1024]{0:T(1024)S(1)} %pad_clamp_fusion.2), kind=kCustom, calls=%fused_computation.1 | custom fusion | bytes 3211296 | tf_op jit(solution)/shard_map/gather | solution.py:102
  49.0 1.7 %broadcast_select_fusion = bf16[8,49,2048]{2,1,0:T(8,128)(2,1)S(1)} fusion(bf16[8,49,2048]{2,1,0:T(8,128)(2,1)} %gather_fusion.1, pred[8]{0:T(512)(128)(4,1)S(1)} %add_compare_fusion), kind=kLoop, calls=%fused_computation.14 | loop fusion | flops 802816 | bytes 3211272 | tf_op jit(solution)/shard_map/jit(_where)/select_n | solution.py:101
  50.7 0.0 copy-start.1
  50.7 2.1 %copy.14 = bf16[8,49,2048]{2,0,1:T(8,128)(2,1)} copy(bf16[8,49,2048]{2,1,0:T(8,128)(2,1)S(1)} %broadcast_select_fusion) | data formatting | bytes 3211264 | tf_op jit(solution)/shard_map/jit(_where)/select_n | solution.py:101
  52.8 2.1 %collective-permute-start = (bf16[8,49,2048]{2,0,1:T(8,128)(2,1)}, bf16[8,49,2048]{2,0,1:T(8,128)(2,1)}, u32[]{:S(2)}, u32[]{:S(2)}) collective-permute-start(bf16[8,49,2048]{2,0,1:T(8,128)(2,1)} %copy.14), channel_id=1, source_target_pairs={{0,1},{1,2},{2,3},{3,4},{4,5},{5,6},{6,7},{7,8},{8,9},{9,10},{10,1... | collective-permute-start | bytes 4816904 | tf_op jit(solution)/shard_map/ppermute | solution.py:13
  54.9 0.0 copy-done.1
  54.9 0.6 gather_fusion.2
  55.6 4.1 %gather_fusion.3 = bf16[8,49,2048]{2,1,0:T(8,128)(2,1)} fusion(bf16[18,49,2048]{2,1,0:T(8,128)(2,1)} %param.12, s32[1024]{0:T(1024)S(1)} %pad_clamp_fusion), kind=kCustom, calls=%fused_computation.3 | custom fusion | bytes 3211296 | tf_op jit(solution)/shard_map/gather | solution.py:105
  59.7 19.1 %collective-permute-done = bf16[8,49,2048]{2,0,1:T(8,128)(2,1)} collective-permute-done((bf16[8,49,2048]{2,0,1:T(8,128)(2,1)}, bf16[8,49,2048]{2,0,1:T(8,128)(2,1)}, u32[]{:S(2)}, u32[]{:S(2)}) %collective-permute-start) | collective-permute-done | bytes 1605664 | tf_op jit(solution)/shard_map/ppermute | solution.py:13
  78.8 5.0 %copy_select_fusion = bf16[8,49,2048]{2,1,0:T(8,128)(2,1)} fusion(bf16[8,49,2048]{2,1,0:T(8,128)(2,1)} %gather_fusion.3, bf16[8,49,2048]{2,0,1:T(8,128)(2,1)} %collective-permute-done, pred[8]{0:T(512)(128)(4,1)S(1)} %iota_compare_fusion), kind=kLoop, calls=%fused_computation.13 | loop fusion | flops 802816 | bytes 4816904 | tf_op jit(solution)/shard_map/jit(_where)/select_n | solution.py:106
  83.7 0.0 copy-start.11
  83.8 3.2 %reshape.114 = bf16[392,2048]{1,0:T(8,128)(2,1)} reshape(bf16[8,49,2048]{2,1,0:T(8,128)(2,1)} %copy_select_fusion) | data formatting | bytes 3211264 | tf_op jit(solution)/shard_map/reshape | solution.py:32
  86.9 0.0 copy-done.11
  86.9 0.0 copy-done.12
  86.9 3.1 %fusion.5 = bf16[392,512]{1,0:T(8,128)(2,1)S(1)} fusion(bf16[392,2048]{1,0:T(8,128)(2,1)} %reshape.114, bf16[2048,512]{1,0:T(8,128)(2,1)} %param.15, f32[512]{0:T(512)S(1)} %copy-done.11, f32[512]{0:T(512)S(1)} %copy-done.12), kind=kOutput, calls=%fused_computation.29 | convolution fusion | flops 822886400 | bytes 4108288 | tf_op jit(solution)/shard_map/dot_general | solution.py:34
  90.0 0.0 copy-start.2
  90.0 0.8 copy-done.2
  90.8 0.9 reshape.115
  91.7 4.9 %pad_slice_fusion = (bf16[8,7,7,512]{3,2,1,0:T(8,128)(2,1)}, bf16[8,7,7,512]{3,2,1,0:T(8,128)(2,1)}, bf16[8,7,7,512]{3,2,1,0:T(8,128)(2,1)}, bf16[8,7,7,512]{3,2...) fusion(bf16[8,7,7,512]{3,2,1,0:T(8,128)(2,1)} %reshape.115), kind=kLoop, calls=%fused_computation.5 | loop fusion | bytes 3612672 | tf_op jit(solution)/shard_map/slice | solution.py:43
  96.6 1.9 %reshape.123 = bf16[392,512]{1,0:T(8,128)(2,1)} reshape(bf16[8,7,7,512]{3,2,1,0:T(8,128)(2,1)} %get-tuple-element.5) | data formatting | bytes 802816 | tf_op jit(solution)/shard_map/reshape | solution.py:45
  98.5 1.9 %reshape.117 = bf16[392,512]{1,0:T(8,128)(2,1)} reshape(bf16[8,7,7,512]{3,2,1,0:T(8,128)(2,1)} %get-tuple-element.6) | data formatting | bytes 802816 | tf_op jit(solution)/shard_map/reshape | solution.py:45
  100.4 1.9 %reshape.118 = bf16[392,512]{1,0:T(8,128)(2,1)} reshape(bf16[8,7,7,512]{3,2,1,0:T(8,128)(2,1)} %get-tuple-element.7) | data formatting | bytes 802816 | tf_op jit(solution)/shard_map/reshape | solution.py:45
  102.3 1.9 %reshape.119 = bf16[392,512]{1,0:T(8,128)(2,1)} reshape(bf16[8,7,7,512]{3,2,1,0:T(8,128)(2,1)} %get-tuple-element.8) | data formatting | bytes 802816 | tf_op jit(solution)/shard_map/reshape | solution.py:45
  104.3 1.9 %reshape.120 = bf16[392,512]{1,0:T(8,128)(2,1)} reshape(bf16[8,7,7,512]{3,2,1,0:T(8,128)(2,1)} %get-tuple-element.9) | data formatting | bytes 802816 | tf_op jit(solution)/shard_map/reshape | solution.py:45
  106.2 0.9 reshape.121
  107.0 0.1 reshape.122
  107.2 0.0 copy-start.8
  107.2 0.9 reshape.116
  108.1 1.6 %fusion.16 = f32[392,512]{1,0:T(8,128)S(1)} fusion(bf16[392,512]{1,0:T(8,128)(2,1)} %reshape.116, bf16[3,3,512,512]{3,2,1,0:T(8,128)(2,1)} %param.18), kind=kOutput, calls=%fused_computation.39 | convolution fusion | flops 205520896 | bytes 1728512 | tf_op jit(solution)/shard_map/dot_general | solution.py:46
  109.7 0.0 copy-done.8
  109.7 0.0 copy-start.6
  109.7 1.5 %convolution_add_fusion.7 = f32[392,512]{1,0:T(8,128)S(1)} fusion(f32[392,512]{1,0:T(8,128)S(1)} %fusion.16, bf16[392,512]{1,0:T(8,128)(2,1)S(1)} %copy-done.8, bf16[3,3,512,512]{3,2,1,0:T(8,128)(2,1)} %param.18), kind=kOutput, calls=%fused_computation.22 | convolution fusion | flops 205721600 | bytes 2531328 | tf_op jit(solution)/shard_map/dot_general | solution.py:46
  111.2 0.0 copy-done.7
  111.2 0.0 copy-start.3
  111.2 1.5 %convolution_add_fusion.6 = f32[392,512]{1,0:T(8,128)S(1)} fusion(f32[392,512]{1,0:T(8,128)S(1)} %convolution_add_fusion.7, bf16[392,512]{1,0:T(8,128)(2,1)S(1)} %copy-done.7, bf16[3,3,512,512]{3,2,1,0:T(8,128)(2,1)} %param.18), kind=kOutput, calls=%fused_computation.21 | convolution fusion | flops 205721600 | bytes 2531328 | tf_op jit(solution)/shard_map/dot_general | solution.py:46
  112.7 0.0 copy-done.6
  112.7 0.0 copy-start.5
  112.7 1.5 %convolution_add_fusion.5 = f32[392,512]{1,0:T(8,128)S(1)} fusion(f32[392,512]{1,0:T(8,128)S(1)} %convolution_add_fusion.6, bf16[392,512]{1,0:T(8,128)(2,1)S(1)} %copy-done.6, bf16[3,3,512,512]{3,2,1,0:T(8,128)(2,1)} %param.18), kind=kOutput, calls=%fused_computation.20 | convolution fusion | flops 205721600 | bytes 2531328 | tf_op jit(solution)/shard_map/dot_general | solution.py:46
  114.2 0.0 copy-done.3
  114.2 0.0 copy-start.4
  114.2 1.5 %convolution_add_fusion.4 = f32[392,512]{1,0:T(8,128)S(1)} fusion(f32[392,512]{1,0:T(8,128)S(1)} %convolution_add_fusion.5, bf16[392,512]{1,0:T(8,128)(2,1)S(1)} %copy-done.3, bf16[3,3,512,512]{3,2,1,0:T(8,128)(2,1)} %param.18), kind=kOutput, calls=%fused_computation.19 | convolution fusion | flops 205721600 | bytes 2531328 | tf_op jit(solution)/shard_map/dot_general | solution.py:46
  115.7 0.0 copy-done.5
  115.7 1.4 %convolution_add_fusion.3 = f32[392,512]{1,0:T(8,128)S(1)} fusion(f32[392,512]{1,0:T(8,128)S(1)} %convolution_add_fusion.4, bf16[392,512]{1,0:T(8,128)(2,1)S(1)} %copy-done.5, bf16[3,3,512,512]{3,2,1,0:T(8,128)(2,1)} %param.18), kind=kOutput, calls=%fused_computation.18 | convolution fusion | flops 205721600 | bytes 2531328 | tf_op jit(solution)/shard_map/dot_general | solution.py:46
  117.1 0.0 copy-done.4
  117.1 0.0 copy-start.9
  117.1 0.0 copy-start.10
  117.1 0.0 copy-start.13
  117.1 0.0 copy-start.14
  117.1 1.4 %convolution_add_fusion.2 = f32[392,512]{1,0:T(8,128)S(1)} fusion(f32[392,512]{1,0:T(8,128)S(1)} %convolution_add_fusion.3, bf16[392,512]{1,0:T(8,128)(2,1)S(1)} %copy-done.4, bf16[3,3,512,512]{3,2,1,0:T(8,128)(2,1)} %param.18), kind=kOutput, calls=%fused_computation.17 | convolution fusion | flops 205721600 | bytes 2531328 | tf_op jit(solution)/shard_map/dot_general | solution.py:46
  118.6 1.4 %convolution_add_fusion.1 = f32[392,512]{1,0:T(8,128)S(1)} fusion(f32[392,512]{1,0:T(8,128)S(1)} %convolution_add_fusion.2, bf16[392,512]{1,0:T(8,128)(2,1)S(1)} %reshape.122, bf16[3,3,512,512]{3,2,1,0:T(8,128)(2,1)} %param.18), kind=kOutput, calls=%fused_computation.16 | convolution fusion | flops 205721600 | bytes 2531328 | tf_op jit(solution)/shard_map/dot_general | solution.py:46
  120.0 0.0 copy-done
  120.0 0.0 copy-done.9
  120.0 0.0 copy-done.10
  120.0 0.0 copy-done.13
  120.0 0.0 copy-done.14
  120.1 4.8 %add_maximum_fusion = f32[392,2048]{1,0:T(8,128)} fusion(bf16[392,2048]{1,0:T(8,128)(2,1)} %reshape.114, bf16[512,2048]{1,0:T(8,128)(2,1)S(1)} %copy-done, f32[2048]{0:T(1024)S(1)} %copy-done.9, f32[2048]{0:T(1024)S(1)} %copy-done.10, f32[392,512]{1,0:T(8,128)S(1)} %convolution_add_fusion.1, bf16[392,512]{1,0:T(8,128)(2,1)} %reshape.123, ...), kind=kOutput, calls=%fused_computation.4 | convolution fusion | flops 1032622080 | bytes 8663040 | tf_op jit(solution)/shard_map/dot_general | solution.py:51
  124.9 4.1 %reshape.124 = f32[8,49,2048]{2,1,0:T(8,128)} reshape(f32[392,2048]{1,0:T(8,128)} %add_maximum_fusion) | data formatting | bytes 6422528 | tf_op jit(solution)/shard_map/reshape | solution.py:57
  129.0 2.5 %reduce_sum.19 = f32[8,2048]{1,0:T(8,128)S(1)} reduce(f32[8,49,2048]{2,1,0:T(8,128)} %reshape.124, f32[]{:T(128)} %constant.8.clone.1), dimensions={1}, to_apply=%region_1.2 | reduce | flops 786432 | bytes 3276804 | tf_op jit(solution)/shard_map/reduce_sum | solution.py:56
  131.4 0.6 multiply_convert_fusion
  (13 shorter events, 0.1 us)
Async XLA Ops:
  0.0 120.0 %copy-start = (bf16[512,2048]{1,0:T(8,128)(2,1)S(1)}, bf16[512,2048]{1,0:T(8,128)(2,1)}, u32[]{:S(2)}) copy-start(bf16[512,2048]{1,0:T(8,128)(2,1)} %param.21) | copy-start | bytes 6291460
  50.7 4.2 %copy-start.1 = (s32[1,18]{1,0:T(1,128)S(1)}, s32[1,18]{1,0:T(1,128)}, u32[]{:S(2)}) copy-start(s32[1,18]{1,0:T(1,128)} %param.13) | copy-start | bytes 220
  52.8 26.0 %collective-permute-start = (bf16[8,49,2048]{2,0,1:T(8,128)(2,1)}, bf16[8,49,2048]{2,0,1:T(8,128)(2,1)}, u32[]{:S(2)}, u32[]{:S(2)}) collective-permute-start(bf16[8,49,2048]{2,0,1:T(8,128)(2,1)} %copy.14), channel_id=1, source_target_pairs={{0,1},{1,2},{2,3},{3,4},{4,5},{5,6},{6,7},{7,8},{8,9},{9,10},{10,1... | collective-permute-start | bytes 4816904 | tf_op jit(solution)/shard_map/ppermute | solution.py:13
  83.7 3.2 %copy-start.11 = (f32[512]{0:T(512)S(1)}, f32[512]{0:T(512)}, u32[]{:S(2)}) copy-start(f32[512]{0:T(512)} %param.17) | copy-start | bytes 6148
  83.8 3.2 %copy-start.12 = (f32[512]{0:T(512)S(1)}, f32[512]{0:T(512)}, u32[]{:S(2)}) copy-start(f32[512]{0:T(512)} %param.16) | copy-start | bytes 6148
  90.0 0.8 copy-start.2
  107.2 2.5 %copy-start.8 = (bf16[392,512]{1,0:T(8,128)(2,1)S(1)}, bf16[392,512]{1,0:T(8,128)(2,1)}, u32[]{:S(2)}) copy-start(bf16[392,512]{1,0:T(8,128)(2,1)} %reshape.117) | copy-start | bytes 1204228
  108.1 3.1 %copy-start.7 = (bf16[392,512]{1,0:T(8,128)(2,1)S(1)}, bf16[392,512]{1,0:T(8,128)(2,1)}, u32[]{:S(2)}) copy-start(bf16[392,512]{1,0:T(8,128)(2,1)} %reshape.118) | copy-start | bytes 1204228
  109.7 3.0 %copy-start.6 = (bf16[392,512]{1,0:T(8,128)(2,1)S(1)}, bf16[392,512]{1,0:T(8,128)(2,1)}, u32[]{:S(2)}) copy-start(bf16[392,512]{1,0:T(8,128)(2,1)} %reshape.119) | copy-start | bytes 1204228
  111.2 3.0 %copy-start.3 = (bf16[392,512]{1,0:T(8,128)(2,1)S(1)}, bf16[392,512]{1,0:T(8,128)(2,1)}, u32[]{:S(2)}) copy-start(bf16[392,512]{1,0:T(8,128)(2,1)} %copy-done.2) | copy-start | bytes 1204228
  112.7 3.0 %copy-start.5 = (bf16[392,512]{1,0:T(8,128)(2,1)S(1)}, bf16[392,512]{1,0:T(8,128)(2,1)}, u32[]{:S(2)}) copy-start(bf16[392,512]{1,0:T(8,128)(2,1)} %reshape.120) | copy-start | bytes 1204228
  114.2 2.9 %copy-start.4 = (bf16[392,512]{1,0:T(8,128)(2,1)S(1)}, bf16[392,512]{1,0:T(8,128)(2,1)}, u32[]{:S(2)}) copy-start(bf16[392,512]{1,0:T(8,128)(2,1)} %reshape.121) | copy-start | bytes 1204228
  117.1 2.9 %copy-start.9 = (f32[2048]{0:T(1024)S(1)}, f32[2048]{0:T(1024)}, u32[]{:S(2)}) copy-start(f32[2048]{0:T(1024)} %param.23) | copy-start | bytes 24580
  117.1 2.9 %copy-start.10 = (f32[2048]{0:T(1024)S(1)}, f32[2048]{0:T(1024)}, u32[]{:S(2)}) copy-start(f32[2048]{0:T(1024)} %param.22) | copy-start | bytes 24580
  117.1 2.9 %copy-start.13 = (f32[512]{0:T(512)S(1)}, f32[512]{0:T(512)}, u32[]{:S(2)}) copy-start(f32[512]{0:T(512)} %param.20) | copy-start | bytes 6148
  117.1 2.9 %copy-start.14 = (f32[512]{0:T(512)S(1)}, f32[512]{0:T(512)}, u32[]{:S(2)}) copy-start(f32[512]{0:T(512)} %param.19) | copy-start | bytes 6148
where the time goes:
time: 133 us; the launch traced here: 132 us
  blocking collectives  41.2 us (31%)
  local copies, waits for them, and re-layouts  37.7 us (28%)
  matrix products  19.6 us (15%)
  waiting for transfers between devices  19.1 us (14%)
  other arithmetic  10.5 us (8%)
  starting transfers between devices  2.09 us (2%)
  between operations  1.83 us (1%)
    unnamed x1, blocking collectives  41.2 us
    ppermute x1, waiting for transfers between devices, passed_along(): return lax.ppermute(x, axis, pairs)  19.1 us
    dot_general x8, matrix products, bottleneck(): jnp.dot(window, w_spatial[row_shift, col_shift], preferred_element_type=j...  11.7 us
    reshape x8, local copies, waits for them, and re-layouts, bottleneck(): window = padded[:, row_shift:row_shift + side_cells, col_shift:col_shift...  11.5 us
    select_n x1, other arithmetic, on_device(): shard_tiles = jnp.where(from_prior[:, None, None], arrived, own_tiles)  4.98 us
    slice x1, local copies, waits for them, and re-layouts, bottleneck(): padded[:, row_shift:row_shift + side_cells, col_shift:col_shift + side_ce...  4.92 us
    dot_general x1, matrix products, bottleneck(): jnp.dot(spatial, w_expand, preferred_element_type=jnp.float32)  4.81 us
    gather x2, local copies, waits for them, and re-layouts, on_device(): own_tiles = tiles[listing[stay_slot]]  4.71 us
  transfers between devices with their start and end apart: 1, of which 1 were waited for; matrix products, arithmetic and copies ran while one was open for 4% of the time, Pallas kernels for 0%

commit v1 on v0

v1 whole, which is shorter than its diff:
```python
import jax
import jax.numpy as jnp
from jax import lax
from jax.experimental import pallas as pl
from jax.experimental.pallas import tpu as pltpu
from jax.sharding import PartitionSpec as P

SIDE = 7
SEQ_DEV = 8
LANES = 128
COLS = 256
AXES = ("grp", "ext")


def encode_body(
    listing,
    count,
    tiles,
    w_reduce,
    scale_reduce,
    bias_reduce,
    w_spatial,
    scale_spatial,
    bias_spatial,
    w_expand,
    scale_expand,
    bias_expand,
    tail,
    head,
    maps,
    w1,
    w2,
    w3,
    last_cell,
    by_cell,
    framed,
    spatial,
    sem,
):
    slots, cells, channels = maps.shape
    inner = w1.shape[1]
    even = cells - 1
    half = slots // 2
    loads = []
    for t in range(slots):
        slot = jnp.clip(count[0] - half + t, 0, slots - 1) if t < half else t - half
        loads.append(pltpu.make_async_copy(tiles.at[listing[0, slot]], maps.at[t], sem.at[t]))
    weights = [
        pltpu.make_async_copy(src, dst, sem.at[slots + i])
        for i, (src, dst) in enumerate(((w_reduce, w1), (w_spatial, w2), (w_expand, w3)))
    ]
    for copy in loads + weights:
        copy.start()
    framed[...] = jnp.zeros(framed.shape, framed.dtype)
    for copy in loads:
        copy.wait()
    for t in range(slots):
        last_cell[t : t + 1, :] = maps[t, even:cells, :].astype(jnp.float32)
    weights[0].wait()
    x_last = last_cell[...].astype(jnp.bfloat16)
    for n in range(0, inner, COLS):
        cols = slice(n, n + COLS)
        w = w1[:, cols]
        most = jnp.dot(
            maps[:, 0:even, :].reshape(slots * even, channels), w, preferred_element_type=jnp.float32
        )
        most = jnp.maximum(most * scale_reduce[:, cols] + bias_reduce[:, cols], 0.0)
        last = jnp.dot(x_last, w, preferred_element_type=jnp.float32)
        last = jnp.maximum(last * scale_reduce[:, cols] + bias_reduce[:, cols], 0.0)
        for q in range(COLS // LANES):
            block = n // LANES + q
            lanes = slice(q * LANES, (q + 1) * LANES)
            for t in range(slots):
                by_cell[block, pl.ds(t, even, stride=slots), :] = most[t * even : (t + 1) * even, lanes]
            by_cell[block, even * slots :, :] = last[:, lanes]
    for i in range(SIDE):
        for block in range(inner // LANES):
            framed[i + 1, slots : slots + SIDE * slots, block * LANES : (block + 1) * LANES] = by_cell[
                block, i * SIDE * slots : (i + 1) * SIDE * slots, :
            ].astype(jnp.bfloat16)
    weights[1].wait()
    for n in range(0, inner, COLS):
        cols = slice(n, n + COLS)
        windows = jnp.concatenate(
            [
                framed[a : a + SIDE, b * slots : (b + SIDE) * slots, :].reshape(cells * slots, inner)
                for a in range(3)
                for b in range(3)
            ],
            axis=1,
        )
        conv = jnp.dot(windows, w2[:, cols], preferred_element_type=jnp.float32)
        conv = jnp.maximum(conv * scale_spatial[:, cols] + bias_spatial[:, cols], 0.0)
        for q in range(COLS // LANES):
            by_cell[n // LANES + q, :, :] = conv[:, q * LANES : (q + 1) * LANES]
    for block in range(inner // LANES):
        lanes = slice(block * LANES, (block + 1) * LANES)
        for t in range(slots):
            spatial[t * even : (t + 1) * even, lanes] = by_cell[
                block, pl.ds(t, even, stride=slots), :
            ].astype(jnp.bfloat16)
        spatial[even * slots :, lanes] = by_cell[block, even * slots :, :].astype(jnp.bfloat16)
    weights[2].wait()
    for n in range(0, channels, COLS):
        cols = slice(n, n + COLS)
        grown = jnp.dot(spatial[...], w3[:, cols], preferred_element_type=jnp.float32)
        grown = grown * scale_expand[:, cols] + bias_expand[:, cols]
        most = grown[: even * slots].reshape(slots, even, COLS) + maps[:, 0:even, cols].astype(jnp.float32)
        last = grown[even * slots :] + last_cell[:, cols]
        total = jnp.sum(jnp.maximum(most, 0.0), axis=1) + jnp.maximum(last, 0.0)
        mean = (total / cells).astype(jnp.bfloat16)
        tail[:, cols] = mean[:half]
        head[:, cols] = mean[half:]


def encode(listing, count, tiles, w_reduce, scale_reduce, bias_reduce, w_spatial, scale_spatial, bias_spatial, w_expand, scale_expand, bias_expand):
    slots = 2 * SEQ_DEV
    cells, channels = tiles.shape[1:]
    inner = w_reduce.shape[1]
    far = pl.BlockSpec(memory_space=pl.ANY)
    near = pl.BlockSpec(memory_space=pltpu.VMEM)
    scalar = pl.BlockSpec(memory_space=pltpu.SMEM)
    row = lambda v: v.reshape(1, -1)
    return pl.pallas_call(
        encode_body,
        out_shape=[jax.ShapeDtypeStruct((SEQ_DEV, channels), jnp.bfloat16)] * 2,
        in_specs=[scalar, scalar, far, far, near, near, far, near, near, far, near, near],
        out_specs=[near, near],
        scratch_shapes=[
            pltpu.VMEM((slots, cells, channels), jnp.bfloat16),
            pltpu.VMEM((channels, inner), jnp.bfloat16),
            pltpu.VMEM((9 * inner, inner), jnp.bfloat16),
            pltpu.VMEM((inner, channels), jnp.bfloat16),
            pltpu.VMEM((slots, channels), jnp.float32),
            pltpu.VMEM((inner // LANES, cells * slots, LANES), jnp.float32),
            pltpu.VMEM((SIDE + 2, (SIDE + 2) * slots, inner), jnp.bfloat16),
            pltpu.VMEM((cells * slots, inner), jnp.bfloat16),
            pltpu.SemaphoreType.DMA((slots + 3,)),
        ],
        cost_estimate=pl.CostEstimate(
            flops=2 * slots * cells * inner * (2 * channels + 9 * inner),
            bytes_accessed=2 * (slots * cells * channels + 2 * channels * inner + 9 * inner * inner),
            transcendentals=0,
        ),
        name="encode",
    )(
        listing,
        count,
        tiles,
        w_reduce,
        row(scale_reduce),
        row(bias_reduce),
        w_spatial.reshape(9 * inner, inner),
        row(scale_spatial),
        row(bias_spatial),
        w_expand,
        row(scale_expand),
        row(bias_expand),
    )


def pack_body(ahead, arrived, head, out, rows):
    half = head.shape[0]
    backlog = jnp.clip(jnp.sum(ahead[...]), 0, half)
    for block in range(rows.shape[0]):
        lanes = slice(block * LANES, (block + 1) * LANES)
        rows[block, :half, :] = arrived[:, lanes].astype(jnp.float32)
        rows[block, half:, :] = head[:, lanes].astype(jnp.float32)
        out[:, lanes] = rows[block, pl.ds(half - backlog, half), :].astype(out.dtype)


def pack(ahead, arrived, head):
    near = pl.BlockSpec(memory_space=pltpu.VMEM)
    return pl.pallas_call(
        pack_body,
        out_shape=jax.ShapeDtypeStruct(head.shape, head.dtype),
        in_specs=[near] * 3,
        out_specs=near,
        scratch_shapes=[pltpu.VMEM((head.shape[1] // LANES, 2 * head.shape[0], LANES), jnp.float32)],
        name="pack",
    )(ahead, arrived, head)


def on_device(tiles, tissue_index, tissue_count, *weights):
    devices = lax.axis_size(AXES)
    rank = lax.axis_index(AXES)
    later = jnp.arange(devices, dtype=jnp.int32) > rank
    adds = jnp.where(later, tissue_count - SEQ_DEV, 0)
    ahead = lax.all_to_all(adds, AXES, 0, 0, tiled=True)
    tail, head = encode(tissue_index, tissue_count, tiles, *weights)
    arrived = lax.ppermute(tail, AXES, [(i, i + 1) for i in range(devices - 1)])
    return pack(ahead.reshape(1, devices), arrived, head)


def solution(mesh):
    owned = P(AXES, None)
    return jax.shard_map(
        on_device,
        mesh=mesh,
        in_specs=(P(AXES, None, None), owned, P(AXES)) + (P(),) * 9,
        out_specs=owned,
        check_vma=False,
    )
```

time: 133 us -> 35.1 us (0.26)
  the two profiles are of different devices: /device:TPU:4 before, /device:TPU:0 now
where the time goes in v1:
time: 35.1 us; the launch traced here: 34.8 us
  Pallas kernels  15.6 us (44%)
  blocking collectives  14 us (40%)
  starting transfers between devices  2.71 us (8%)
  other arithmetic  1.2 us (3%)
  between operations  0.69 us (2%)
  local copies, waits for them, and re-layouts  0.61 us (2%)
    all_to_all x1, blocking collectives, on_device(): ahead = lax.all_to_all(adds, AXES, 0, 0, tiled=True)  14 us
    pallas_call x1, Pallas kernels, encode(): pl.pallas_call(encode_body, out_shape=[jax.ShapeDtypeStruct((SEQ_DEV, cha...  14 us
    ppermute x1, starting transfers between devices, on_device(): arrived = lax.ppermute(tail, AXES, [(i, i + 1) for i in range(devices - 1)])  2.71 us
    pallas_call x1, Pallas kernels, pack(): pl.pallas_call(pack_body, out_shape=jax.ShapeDtypeStruct(head.shape, head...  1.61 us
    all_to_all x1, other arithmetic, on_device(): ahead = lax.all_to_all(adds, AXES, 0, 0, tiled=True)  1.18 us
  transfers between devices with their start and end apart: 1, of which 0 were waited for; matrix products, arithmetic and copies ran while one was open for 3% of the time, Pallas kernels for 0%

profile of v1, /device:TPU:0, one launch (start us, length us, event | category | flops | bytes accessed | tf_op | source)
XLA Modules:
  0.0 34.8 jit_solution(3175272110607801946)
XLA Ops:
  0.7 14.0 %encode.1 = (bf16[8,2048]{1,0:T(8,128)(2,1)}, bf16[8,2048]{1,0:T(8,128)(2,1)}) custom-call(s32[1,18]{1,0:T(1,128)} %listing.1, s32[1]{0:T(128)S(6)} %copy.13.count, bf16[18,49,2048]{2,1,0:T(8,128)(2,1)} %tiles.1, bf16[2048,512]{1,0:T(8,128)(2,1)} %w_reduce.1, f32[1,512]{1,0:T(1,128)} %bitcast.13, f32[1,512]{1,0:T(1,128)} %bitcast.14, ...), custom_call_target="tpu_custom_call" | custom-call | flops 6987710464 | bytes 12124160 | tf_op jit(solution)/shard_map/encode/pallas_call | solution.py:124
  14.6 2.7 %collective-permute-start = (bf16[8,2048]{1,0:T(8,128)(2,1)}, bf16[8,2048]{1,0:T(8,128)(2,1)S(1)}, u32[]{:S(2)}, u32[]{:S(2)}) collective-permute-start(bf16[8,2048]{1,0:T(8,128)(2,1)} %get-tuple-element.7), channel_id=1, source_target_pairs={{0,1},{1,2},{2,3},{3,4},{4,5},{5,6},{6,7},{7,8},{8,9},{9,10},{10,1... | collective-permute-start | bytes 98312 | tf_op jit(solution)/shard_map/ppermute | solution.py:191
  17.4 14.0 %all_to_all.6 = s32[32,1,1]{2,1,0:T(1,128)S(1)} all-to-all(s32[32,1,1]{2,1,0:T(1,128)S(1)} %compare_select_fusion), channel_id=1, replica_groups=mesh['grp'=4,'ext'=8] {'grp','ext'}, dimensions={0} | all-to-all | bytes 256 | tf_op jit(solution)/shard_map/all_to_all | solution.py:189
  31.4 1.2 %reduce = s32[32]{0:T(128)} reduce(s32[32,1,1]{2,1,0:T(1,128)S(1)} %all_to_all.6, s32[]{:T(128)} %constant.14.clone.1), dimensions={1,2}, to_apply=%all_to_all.4.reduce_sub_computation | reduce | bytes 260 | tf_op jit(solution)/shard_map/all_to_all | solution.py:189
  32.6 0.0 collective-permute-done.arrived
  32.6 0.0 copy-start
  32.6 0.6 %copy-done = bf16[8,2048]{1,0:T(8,128)(2,1)} copy-done((bf16[8,2048]{1,0:T(8,128)(2,1)}, bf16[8,2048]{1,0:T(8,128)(2,1)S(1)}, u32[]{:S(2)}) %copy-start) | copy-done | bytes 32792
  33.2 1.6 %pack.1 = bf16[8,2048]{1,0:T(8,128)(2,1)} custom-call(s32[1,32]{1,0:T(1,128)} %bitcast.9, bf16[8,2048]{1,0:T(8,128)(2,1)} %copy-done, bf16[8,2048]{1,0:T(8,128)(2,1)} %get-tuple-element.8.head), custom_call_target="tpu_custom_call" | custom-call | tf_op jit(solution)/shard_map/pack/pallas_call | solution.py:174
  (1 shorter events, 0.0 us)
Async XLA Ops:
  14.6 17.9 %collective-permute-start = (bf16[8,2048]{1,0:T(8,128)(2,1)}, bf16[8,2048]{1,0:T(8,128)(2,1)S(1)}, u32[]{:S(2)}, u32[]{:S(2)}) collective-permute-start(bf16[8,2048]{1,0:T(8,128)(2,1)} %get-tuple-element.7), channel_id=1, source_target_pairs={{0,1},{1,2},{2,3},{3,4},{4,5},{5,6},{6,7},{7,8},{8,9},{9,10},{10,1... | collective-permute-start | bytes 98312 | tf_op jit(solution)/shard_map/ppermute | solution.py:191
  32.6 0.6 %copy-start = (bf16[8,2048]{1,0:T(8,128)(2,1)}, bf16[8,2048]{1,0:T(8,128)(2,1)S(1)}, u32[]{:S(2)}) copy-start(bf16[8,2048]{1,0:T(8,128)(2,1)S(1)} %collective-permute-done.arrived) | copy-start | bytes 98308

commit v2 on v1

v2 whole, which is shorter than its diff:
```python
import jax
import jax.numpy as jnp
from jax import lax
from jax.experimental import pallas as pl
from jax.experimental.pallas import tpu as pltpu
from jax.sharding import PartitionSpec as P


SIDE = 7
SEQ_DEV = 8
LANES = 128
COLS = 256
AXES = ("grp", "ext")
SCALAR = pl.BlockSpec(memory_space=pltpu.SMEM)
NEAR = pl.BlockSpec(memory_space=pltpu.VMEM)
FAR = pl.BlockSpec(memory_space=pltpu.HBM)


def held(value):
    return pltpu.with_memory_space_constraint(value, pltpu.VMEM)


def encode(maps, weights, out, last_cell, by_cell, framed, spatial, ready=lambda stage: None):
    w_reduce, scale_reduce, bias_reduce, w_spatial, scale_spatial, bias_spatial, w_expand, scale_expand, bias_expand = weights
    count, cells, channels = maps.shape
    inner = w_reduce.shape[1]
    even = cells - 1
    framed[...] = jnp.zeros(framed.shape, framed.dtype)
    ready(0)
    for t in range(count):
        last_cell[t : t + 1, :] = maps[t, even:cells, :].astype(jnp.float32)
    x_last = last_cell[...].astype(jnp.bfloat16)
    for n in range(0, inner, COLS):
        cols = slice(n, n + COLS)
        w = w_reduce[:, cols]
        most = jnp.dot(maps[:, 0:even, :].reshape(count * even, channels), w, preferred_element_type=jnp.float32)
        most = jnp.maximum(most * scale_reduce[:, cols] + bias_reduce[:, cols], 0.0)
        last = jnp.dot(x_last, w, preferred_element_type=jnp.float32)
        last = jnp.maximum(last * scale_reduce[:, cols] + bias_reduce[:, cols], 0.0)
        for q in range(COLS // LANES):
            block = n // LANES + q
            lanes = slice(q * LANES, (q + 1) * LANES)
            for t in range(count):
                by_cell[block, pl.ds(t, even, stride=count), :] = most[t * even : (t + 1) * even, lanes]
            by_cell[block, even * count :, :] = last[:, lanes]
    for i in range(SIDE):
        for block in range(inner // LANES):
            framed[i + 1, count : count + SIDE * count, block * LANES : (block + 1) * LANES] = by_cell[
                block, i * SIDE * count : (i + 1) * SIDE * count, :
            ].astype(jnp.bfloat16)
    ready(1)
    for n in range(0, inner, COLS):
        cols = slice(n, n + COLS)
        windows = jnp.concatenate(
            [
                framed[a : a + SIDE, b * count : (b + SIDE) * count, :].reshape(cells * count, inner)
                for a in range(3)
                for b in range(3)
            ],
            axis=1,
        )
        conv = jnp.dot(windows, w_spatial[:, cols], preferred_element_type=jnp.float32)
        conv = jnp.maximum(conv * scale_spatial[:, cols] + bias_spatial[:, cols], 0.0)
        for q in range(COLS // LANES):
            by_cell[n // LANES + q, :, :] = conv[:, q * LANES : (q + 1) * LANES]
    for block in range(inner // LANES):
        lanes = slice(block * LANES, (block + 1) * LANES)
        for t in range(count):
            spatial[t * even : (t + 1) * even, lanes] = by_cell[block, pl.ds(t, even, stride=count), :].astype(
                jnp.bfloat16
            )
        spatial[even * count :, lanes] = by_cell[block, even * count :, :].astype(jnp.bfloat16)
    ready(2)
    for n in range(0, channels, COLS):
        cols = slice(n, n + COLS)
        grown = jnp.dot(spatial[...], w_expand[:, cols], preferred_element_type=jnp.float32)
        grown = grown * scale_expand[:, cols] + bias_expand[:, cols]
        most = grown[: even * count].reshape(count, even, COLS) + maps[:, 0:even, cols].astype(jnp.float32)
        last = grown[even * count :] + last_cell[:, cols]
        total = jnp.sum(jnp.maximum(most, 0.0), axis=1) + jnp.maximum(last, 0.0)
        out[:, cols] = (total / cells).astype(out.dtype)


def scratch(cells, channels, inner):
    return [
        pltpu.VMEM((SEQ_DEV, channels), jnp.float32),
        pltpu.VMEM((inner // LANES, cells * SEQ_DEV, LANES), jnp.float32),
        pltpu.VMEM((SIDE + 2, (SIDE + 2) * SEQ_DEV, inner), jnp.bfloat16),
        pltpu.VMEM((cells * SEQ_DEV, inner), jnp.bfloat16),
    ]


def cost(cells, channels, inner):
    return pl.CostEstimate(
        flops=2 * SEQ_DEV * cells * inner * (2 * channels + 9 * inner),
        bytes_accessed=2 * (SEQ_DEV * cells * channels + 2 * channels * inner + 9 * inner * inner),
        transcendentals=0,
    )


def tail_body(listing, count, tiles, w_spatial_far, w_expand_far, w_reduce, s1, b1, s2, b2, s3, b3, tail, head_maps, w_spatial, w_expand, maps, *rest):
    *work, sem = rest
    own = maps.shape[0]
    loads = []
    for t in range(own):
        slot = jnp.clip(count[0, 0] - own + t, 0, 2 * own - 1)
        loads.append(pltpu.make_async_copy(tiles.at[listing[0, slot]], maps.at[t], sem.at[t]))
    later = [
        pltpu.make_async_copy(w_spatial_far, w_spatial, sem.at[own]),
        pltpu.make_async_copy(w_expand_far, w_expand, sem.at[own + 1]),
    ]
    later += [
        pltpu.make_async_copy(tiles.at[listing[0, t]], head_maps.at[t], sem.at[own + 2 + t]) for t in range(own)
    ]
    for copy in loads + later:
        copy.start()

    def ready(stage):
        if stage == 0:
            for copy in loads:
                copy.wait()
        else:
            later[stage - 1].wait()

    encode(maps, (w_reduce, s1, b1, w_spatial, s2, b2, w_expand, s3, b3), tail, *work, ready=ready)
    for copy in later[2:]:
        copy.wait()


def encode_tail(listing, count, tiles, w_reduce, s1, b1, w_spatial, s2, b2, w_expand, s3, b3):
    cells, channels = tiles.shape[1:]
    inner = w_reduce.shape[1]
    maps = (SEQ_DEV, cells, channels)
    return pl.pallas_call(
        tail_body,
        out_shape=[
            pltpu.VMEM((SEQ_DEV, channels), jnp.bfloat16),
            pltpu.VMEM(maps, tiles.dtype),
            pltpu.VMEM(w_spatial.shape, w_spatial.dtype),
            pltpu.VMEM(w_expand.shape, w_expand.dtype),
        ],
        in_specs=[SCALAR] * 2 + [FAR] * 3 + [NEAR] * 7,
        out_specs=[NEAR] * 4,
        scratch_shapes=[pltpu.VMEM(maps, tiles.dtype)]
        + scratch(cells, channels, inner)
        + [pltpu.SemaphoreType.DMA((2 * SEQ_DEV + 2,))],
        cost_estimate=cost(cells, channels, inner),
        compiler_params=pltpu.CompilerParams(vmem_limit_bytes=40 << 20),
        name="encode_tail",
    )(listing, count, *(pltpu.with_memory_space_constraint(v, pltpu.HBM) for v in (tiles, w_spatial, w_expand)), w_reduce, s1, b1, s2, b2, s3, b3)


def head_body(maps, w_reduce, s1, b1, w_spatial, s2, b2, w_expand, s3, b3, head, *work):
    encode(maps, (w_reduce, s1, b1, w_spatial, s2, b2, w_expand, s3, b3), head, *work)


def encode_head(maps, *weights):
    cells, channels = maps.shape[1:]
    inner = weights[0].shape[1]
    return pl.pallas_call(
        head_body,
        out_shape=pltpu.VMEM((SEQ_DEV, channels), jnp.bfloat16),
        in_specs=[NEAR] * 10,
        out_specs=NEAR,
        scratch_shapes=scratch(cells, channels, inner),
        cost_estimate=cost(cells, channels, inner),
        compiler_params=pltpu.CompilerParams(vmem_limit_bytes=24 << 20),
        name="encode_head",
    )(maps, *weights)


def pack_body(ahead, arrived, head, out, rows):
    half = head.shape[0]
    backlog = jnp.clip(jnp.sum(ahead[...]) // LANES, 0, half)
    for block in range(rows.shape[0]):
        lanes = slice(block * LANES, (block + 1) * LANES)
        rows[block, :half, :] = arrived[:, lanes].astype(jnp.float32)
        rows[block, half:, :] = head[:, lanes].astype(jnp.float32)
        out[:, lanes] = rows[block, pl.ds(half - backlog, half), :].astype(out.dtype)


def pack(ahead, arrived, head):
    return pl.pallas_call(
        pack_body,
        out_shape=jax.ShapeDtypeStruct(head.shape, head.dtype),
        in_specs=[NEAR] * 3,
        out_specs=NEAR,
        scratch_shapes=[pltpu.VMEM((head.shape[1] // LANES, 2 * head.shape[0], LANES), jnp.float32)],
        compiler_params=pltpu.CompilerParams(vmem_limit_bytes=4 << 20),
        name="pack",
    )(held(ahead), held(arrived), held(head))


def spread_body(where, count, out):
    place = lax.broadcasted_iota(jnp.int32, out.shape, 0)
    out[...] = jnp.where(place > where[0, 0], count[0, 0] - SEQ_DEV, 0)


def spread(where, count, devices):
    return pl.pallas_call(
        spread_body,
        out_shape=jax.ShapeDtypeStruct((devices, 1, LANES), jnp.int32),
        in_specs=[SCALAR] * 2,
        out_specs=NEAR,
        cost_estimate=pl.CostEstimate(flops=10**11, bytes_accessed=10**8, transcendentals=0),
        compiler_params=pltpu.CompilerParams(vmem_limit_bytes=1 << 20),
        name="spread",
    )(where, count)


def on_device(tiles, tissue_index, tissue_count, w_reduce, s1, b1, w_spatial, s2, b2, w_expand, s3, b3):
    devices = lax.axis_size(AXES)
    rank = lax.axis_index(AXES).reshape(1, 1)
    count = tissue_count.reshape(1, 1)
    inner = w_reduce.shape[1]
    w_spatial = w_spatial.reshape(9 * inner, inner)
    w_reduce, s1, b1, s2, b2, s3, b3 = (
        held(v.reshape(-1, v.shape[-1])) for v in (w_reduce, s1, b1, s2, b2, s3, b3)
    )
    ahead = lax.all_to_all(spread(rank, count, devices), AXES, 0, 0, tiled=True)
    tail, maps, w_spatial, w_expand = encode_tail(
        tissue_index, count, tiles, w_reduce, s1, b1, w_spatial, s2, b2, w_expand, s3, b3
    )
    arrived = lax.ppermute(tail, AXES, [(i, i + 1) for i in range(devices - 1)])
    head = encode_head(maps, w_reduce, s1, b1, w_spatial, s2, b2, w_expand, s3, b3)
    return pack(ahead, arrived, head)


def solution(mesh):
    owned = P(AXES, None)
    return jax.shard_map(
        on_device,
        mesh=mesh,
        in_specs=(P(AXES, None, None), owned, P(AXES)) + (P(),) * 9,
        out_specs=owned,
        check_vma=False,
    )
```

time: 35.1 us -> 42.2 us (1.20)
  local copies, waits for them, and re-layouts: 0.61 us -> 16.6 us
  blocking collectives: 14 us -> 0 us
  starting transfers between devices: 2.71 us -> 10.7 us
  Pallas kernels: 15.6 us -> 13.5 us
  other arithmetic: 1.2 us -> 0 us
    unnamed x2 -> x42, local copies, waits for them, and re-layouts: 0.61 us -> 16.6 us
    all_to_all x1 -> x0, blocking collectives: 14 us -> none  [on_device(): ahead = lax.all_to_all(adds, AXES, 0, 0, tiled=True)]
    all_to_all x0 -> x1, starting transfers between devices: none -> 8.33 us  [on_device(): ahead = lax.all_to_all(spread(rank, count, devices), AXES, 0, 0, tiled=True)]
    pallas_call x1 -> x3, Pallas kernels: 14 us -> 12.6 us  [the longest x1 7.37 us: encode_tail(): pl.pallas_call(tail_body, out_shape=[pltpu.VMEM((SEQ_DEV, channels), jnp....]
    all_to_all x1 -> x0, other arithmetic: 1.18 us -> none  [on_device(): ahead = lax.all_to_all(adds, AXES, 0, 0, tiled=True)]
    pallas_call x1, Pallas kernels: 1.61 us -> 0.85 us  [pack(): pl.pallas_call(pack_body, out_shape=jax.ShapeDtypeStruct(head.shape, head...]
  transfers between devices with their start and end apart: 1 -> 2, of which waited for: 0 -> 0; matrix products, arithmetic and copies ran while one was open for 3% -> 0% of each run, Pallas kernels for 0% -> 13%
where the time goes in v2:
time: 42.2 us; the launch traced here: 41.7 us
  local copies, waits for them, and re-layouts  16.6 us (39%)
  Pallas kernels  13.5 us (32%)
  starting transfers between devices  10.7 us (25%)
  between operations  0.85 us (2%)
    unnamed x42, local copies, waits for them, and re-layouts  16.6 us
    all_to_all x1, starting transfers between devices, on_device(): ahead = lax.all_to_all(spread(rank, count, devices), AXES, 0, 0, tiled=True)  8.33 us
    pallas_call x1, Pallas kernels, encode_tail(): pl.pallas_call(tail_body, out_shape=[pltpu.VMEM((SEQ_DEV, channels), jnp....  7.37 us
    pallas_call x1, Pallas kernels, encode_head(): pl.pallas_call(head_body, out_shape=pltpu.VMEM((SEQ_DEV, channels), jnp.b...  4.63 us
    ppermute x1, starting transfers between devices, on_device(): arrived = lax.ppermute(tail, AXES, [(i, i + 1) for i in range(devices - 1)])  2.39 us
    pallas_call x1, Pallas kernels, pack(): pl.pallas_call(pack_body, out_shape=jax.ShapeDtypeStruct(head.shape, head...  0.85 us
  transfers between devices with their start and end apart: 2, of which 0 were waited for; matrix products, arithmetic and copies ran while one was open for 0% of the time, Pallas kernels for 13%

profile of v2, /device:TPU:0, one launch (start us, length us, event | category | flops | bytes accessed | tf_op | source)
XLA Modules:
  0.0 41.7 jit_solution(14110503160216141496)
XLA Ops:
  0.7 0.0 copy-start
  0.7 1.6 %copy-done = bf16[2048,512]{1,0:T(8,128)(2,1)S(1)} copy-done((bf16[2048,512]{1,0:T(8,128)(2,1)S(1)}, bf16[2048,512]{1,0:T(8,128)(2,1)}, u32[]{:S(2)}) %copy-start) | copy-done | bytes 2097176
  2.2 0.0 copy-start.2
  2.2 0.7 %copy-done.2 = f32[2048]{0:T(1024)S(1)} copy-done((f32[2048]{0:T(1024)S(1)}, f32[2048]{0:T(1024)}, u32[]{:S(2)}) %copy-start.2) | copy-done | bytes 8216
  2.9 0.0 copy-start.4
  2.9 0.7 %copy-done.4 = f32[2048]{0:T(1024)S(1)} copy-done((f32[2048]{0:T(1024)S(1)}, f32[2048]{0:T(1024)}, u32[]{:S(2)}) %copy-start.4) | copy-done | bytes 8216
  3.6 0.0 copy-start.6
  3.6 0.7 %copy-done.6 = f32[512]{0:T(512)S(1)} copy-done((f32[512]{0:T(512)S(1)}, f32[512]{0:T(512)}, u32[]{:S(2)}) %copy-start.6) | copy-done | bytes 2072
  4.3 0.0 copy-start.8
  4.3 0.7 %copy-done.8 = f32[512]{0:T(512)S(1)} copy-done((f32[512]{0:T(512)S(1)}, f32[512]{0:T(512)}, u32[]{:S(2)}) %copy-start.8) | copy-done | bytes 2072
  5.0 0.0 copy-start.10
  5.0 0.7 %copy-done.10 = f32[512]{0:T(512)S(1)} copy-done((f32[512]{0:T(512)S(1)}, f32[512]{0:T(512)}, u32[]{:S(2)}) %copy-start.10) | copy-done | bytes 2072
  5.7 0.0 copy-start.12
  5.7 0.7 %copy-done.12 = f32[512]{0:T(512)S(1)} copy-done((f32[512]{0:T(512)S(1)}, f32[512]{0:T(512)}, u32[]{:S(2)}) %copy-start.12) | copy-done | bytes 2072
  6.4 0.0 copy-start.14
  6.4 0.7 %copy-done.14 = s32[1,18]{1,0:T(1,128)S(1)} copy-done((s32[1,18]{1,0:T(1,128)S(1)}, s32[1,18]{1,0:T(1,128)}, u32[]{:S(2)}) %copy-start.14) | copy-done | bytes 96
  7.0 7.4 %encode_tail.1 = (bf16[8,2048]{1,0:T(8,128)(2,1)S(1)}, bf16[8,49,2048]{2,1,0:T(8,128)(2,1)S(1)}, bf16[4608,512]{1,0:T(8,128)(2,1)S(1)}, bf16[512,2048]{1,0:T(8,128)(2,1)S(1)}) custom-call(s32[1,18]{1,0:T(1,128)S(1)} %copy-done.14, s32[1,1]{1,0:T(1,128)} %bitcast.10.count, bf16[18,49,2048]{2,1,0:T(8,128)(2,1)} %tiles.1, bf16[4608,512]{1,0:T(8,128)(2,1)} %bitcast.23, ...), custom_call_target="tpu_custom_call" | custom-call | flops 3493855232 | bytes 10518528 | tf_op jit(solution)/shard_map/encode_tail/pallas_call | solution.py:134
  14.4 0.0 copy-start.15
  14.4 2.1 %copy-done.15 = bf16[4608,512]{1,0:T(8,128)(2,1)} copy-done((bf16[4608,512]{1,0:T(8,128)(2,1)}, bf16[4608,512]{1,0:T(8,128)(2,1)S(1)}, u32[]{:S(2)}) %copy-start.15) | copy-done | bytes 4718616
  16.5 0.0 copy-start.17
  16.5 1.4 %copy-done.17 = bf16[512,2048]{1,0:T(8,128)(2,1)} copy-done((bf16[512,2048]{1,0:T(8,128)(2,1)}, bf16[512,2048]{1,0:T(8,128)(2,1)S(1)}, u32[]{:S(2)}) %copy-start.17) | copy-done | bytes 2097176
  17.9 0.0 copy-start.19
  17.9 1.3 %copy-done.19 = bf16[8,49,2048]{2,1,0:T(8,128)(2,1)} copy-done((bf16[8,49,2048]{2,1,0:T(8,128)(2,1)}, bf16[8,49,2048]{2,1,0:T(8,128)(2,1)S(1)}, u32[]{:S(2)}) %copy-start.19) | copy-done | bytes 1605656
  19.2 2.4 %collective-permute-start = (bf16[8,2048]{1,0:T(8,128)(2,1)S(1)}, bf16[8,2048]{1,0:T(8,128)(2,1)S(1)}, u32[]{:S(2)}, u32[]{:S(2)}) collective-permute-start(bf16[8,2048]{1,0:T(8,128)(2,1)S(1)} %get-tuple-element.9), channel_id=1, source_target_pairs={{0,1},{1,2},{2,3},{3,4},{4,5},{5,6},{6,7},{7,8},{8,9},{9,10},{10,1... | collective-permute-start | bytes 98312 | tf_op jit(solution)/shard_map/ppermute | solution.py:224
  21.6 0.0 copy-start.1
  21.6 0.0 copy-start.3
  21.6 0.0 copy-start.5
  21.7 0.0 copy-start.7
  21.7 0.0 copy-start.9
  21.7 0.0 copy-start.11
  21.7 0.0 copy-start.13
  21.7 0.6 %spread.1 = s32[32,1,128]{2,1,0:T(1,128)} custom-call(s32[1,1]{1,0:T(1,128)} %bitcast.where, s32[1,1]{1,0:T(1,128)} %bitcast.9.count), custom_call_target="tpu_custom_call" | custom-call | flops 99999997952 | bytes 100000000 | tf_op jit(solution)/shard_map/spread/pallas_call | solution.py:200
  22.3 8.3 %all-to-all-start = ((s32[32,1,128]{2,1,0:T(1,128)}), s32[32,1,128]{2,1,0:T(1,128)S(1)}, u32[]{:S(2)}, u32[]{:S(2)}) async-start(s32[32,1,128]{2,1,0:T(1,128)} %spread.1), calls=%async_computation | async-start | bytes 32768 | tf_op jit(solution)/shard_map/all_to_all | solution.py:220
  30.7 0.0 copy-done.1
  30.7 0.0 copy-done.3
  30.7 0.0 copy-done.5
  30.7 0.0 copy-done.7
  30.7 0.0 copy-done.9
  30.7 0.0 copy-done.11
  30.7 0.0 copy-done.13
  30.7 0.0 copy-start.16
  30.7 2.3 %copy-done.16 = bf16[4608,512]{1,0:T(8,128)(2,1)S(1)} copy-done((bf16[4608,512]{1,0:T(8,128)(2,1)S(1)}, bf16[4608,512]{1,0:T(8,128)(2,1)}, u32[]{:S(2)}) %copy-start.16) | copy-done | bytes 4718616
  33.1 0.0 copy-start.18
  33.1 1.6 %copy-done.18 = bf16[512,2048]{1,0:T(8,128)(2,1)S(1)} copy-done((bf16[512,2048]{1,0:T(8,128)(2,1)S(1)}, bf16[512,2048]{1,0:T(8,128)(2,1)}, u32[]{:S(2)}) %copy-start.18) | copy-done | bytes 2097176
  34.7 0.0 copy-start.20
  34.7 1.5 %copy-done.20 = bf16[8,49,2048]{2,1,0:T(8,128)(2,1)S(1)} copy-done((bf16[8,49,2048]{2,1,0:T(8,128)(2,1)S(1)}, bf16[8,49,2048]{2,1,0:T(8,128)(2,1)}, u32[]{:S(2)}) %copy-start.20) | copy-done | bytes 1605656
  36.2 4.6 %encode_head.1.head = bf16[8,2048]{1,0:T(8,128)(2,1)S(1)} custom-call(bf16[8,49,2048]{2,1,0:T(8,128)(2,1)S(1)} %copy-done.20, bf16[2048,512]{1,0:T(8,128)(2,1)S(1)} %copy-done.1, f32[1,512]{1,0:T(1,128)S(1)} %bitcast.16, f32[1,512]{1,0:T(1,128)S(1)} %bitcast.18, bf16[4608,512]{1,0:T(8,128)(2,1)S(1)} %copy-done.16, f32[1,512]{1,0:T(1,128)S(1)} %bitcast.20, ...), custom_call_target="tpu_custom_call" | custom-call | flops 3493855232 | bytes 10518528 | tf_op jit(solution)/shard_map/encode_head/pallas_call | solution.py:160
  40.8 0.0 all-to-all-done.ahead
  40.8 0.0 collective-permute-done.arrived
  40.8 0.8 %pack.1 = bf16[8,2048]{1,0:T(8,128)(2,1)} custom-call(s32[32,1,128]{2,1,0:T(1,128)S(1)} %all-to-all-done.ahead, bf16[8,2048]{1,0:T(8,128)(2,1)S(1)} %collective-permute-done.arrived, bf16[8,2048]{1,0:T(8,128)(2,1)S(1)} %encode_head.1.head), custom_call_target="tpu_custom_call" | custom-call | tf_op jit(solution)/shard_map/pack/pallas_call | solution.py:183
Async XLA Ops:
  0.7 1.6 %copy-start = (bf16[2048,512]{1,0:T(8,128)(2,1)S(1)}, bf16[2048,512]{1,0:T(8,128)(2,1)}, u32[]{:S(2)}) copy-start(bf16[2048,512]{1,0:T(8,128)(2,1)} %w_reduce.3) | copy-start | bytes 6291460
  2.2 0.7 %copy-start.2 = (f32[2048]{0:T(1024)S(1)}, f32[2048]{0:T(1024)}, u32[]{:S(2)}) copy-start(f32[2048]{0:T(1024)} %param.22) | copy-start | bytes 24580
  2.9 0.7 %copy-start.4 = (f32[2048]{0:T(1024)S(1)}, f32[2048]{0:T(1024)}, u32[]{:S(2)}) copy-start(f32[2048]{0:T(1024)} %param.23) | copy-start | bytes 24580
  3.6 0.7 %copy-start.6 = (f32[512]{0:T(512)S(1)}, f32[512]{0:T(512)}, u32[]{:S(2)}) copy-start(f32[512]{0:T(512)} %param.16) | copy-start | bytes 6148
  4.3 0.7 %copy-start.8 = (f32[512]{0:T(512)S(1)}, f32[512]{0:T(512)}, u32[]{:S(2)}) copy-start(f32[512]{0:T(512)} %param.17) | copy-start | bytes 6148
  5.0 0.7 %copy-start.10 = (f32[512]{0:T(512)S(1)}, f32[512]{0:T(512)}, u32[]{:S(2)}) copy-start(f32[512]{0:T(512)} %param.19) | copy-start | bytes 6148
  5.7 0.7 %copy-start.12 = (f32[512]{0:T(512)S(1)}, f32[512]{0:T(512)}, u32[]{:S(2)}) copy-start(f32[512]{0:T(512)} %param.20) | copy-start | bytes 6148
  6.4 0.7 %copy-start.14 = (s32[1,18]{1,0:T(1,128)S(1)}, s32[1,18]{1,0:T(1,128)}, u32[]{:S(2)}) copy-start(s32[1,18]{1,0:T(1,128)} %listing.1) | copy-start | bytes 220
  14.4 2.1 %copy-start.15 = (bf16[4608,512]{1,0:T(8,128)(2,1)}, bf16[4608,512]{1,0:T(8,128)(2,1)S(1)}, u32[]{:S(2)}) copy-start(bf16[4608,512]{1,0:T(8,128)(2,1)S(1)} %get-tuple-element.11.w_spatial) | copy-start | bytes 14155780
  16.5 1.4 %copy-start.17 = (bf16[512,2048]{1,0:T(8,128)(2,1)}, bf16[512,2048]{1,0:T(8,128)(2,1)S(1)}, u32[]{:S(2)}) copy-start(bf16[512,2048]{1,0:T(8,128)(2,1)S(1)} %get-tuple-element.12.w_expand) | copy-start | bytes 6291460
  17.9 1.3 %copy-start.19 = (bf16[8,49,2048]{2,1,0:T(8,128)(2,1)}, bf16[8,49,2048]{2,1,0:T(8,128)(2,1)S(1)}, u32[]{:S(2)}) copy-start(bf16[8,49,2048]{2,1,0:T(8,128)(2,1)S(1)} %get-tuple-element.10.maps) | copy-start | bytes 4816900
  19.2 21.6 %collective-permute-start = (bf16[8,2048]{1,0:T(8,128)(2,1)S(1)}, bf16[8,2048]{1,0:T(8,128)(2,1)S(1)}, u32[]{:S(2)}, u32[]{:S(2)}) collective-permute-start(bf16[8,2048]{1,0:T(8,128)(2,1)S(1)} %get-tuple-element.9), channel_id=1, source_target_pairs={{0,1},{1,2},{2,3},{3,4},{4,5},{5,6},{6,7},{7,8},{8,9},{9,10},{10,1... | collective-permute-start | bytes 98312 | tf_op jit(solution)/shard_map/ppermute | solution.py:224
  21.6 9.0 %copy-start.1 = (bf16[2048,512]{1,0:T(8,128)(2,1)S(1)}, bf16[2048,512]{1,0:T(8,128)(2,1)}, u32[]{:S(2)}) copy-start(bf16[2048,512]{1,0:T(8,128)(2,1)} %w_reduce.3) | copy-start | bytes 6291460
  21.6 9.0 %copy-start.3 = (f32[2048]{0:T(1024)S(1)}, f32[2048]{0:T(1024)}, u32[]{:S(2)}) copy-start(f32[2048]{0:T(1024)} %param.22) | copy-start | bytes 24580
  21.6 9.0 %copy-start.5 = (f32[2048]{0:T(1024)S(1)}, f32[2048]{0:T(1024)}, u32[]{:S(2)}) copy-start(f32[2048]{0:T(1024)} %param.23) | copy-start | bytes 24580
  21.7 9.0 %copy-start.7 = (f32[512]{0:T(512)S(1)}, f32[512]{0:T(512)}, u32[]{:S(2)}) copy-start(f32[512]{0:T(512)} %param.16) | copy-start | bytes 6148
  21.7 9.0 %copy-start.9 = (f32[512]{0:T(512)S(1)}, f32[512]{0:T(512)}, u32[]{:S(2)}) copy-start(f32[512]{0:T(512)} %param.17) | copy-start | bytes 6148
  21.7 9.0 %copy-start.11 = (f32[512]{0:T(512)S(1)}, f32[512]{0:T(512)}, u32[]{:S(2)}) copy-start(f32[512]{0:T(512)} %param.19) | copy-start | bytes 6148
  21.7 9.0 %copy-start.13 = (f32[512]{0:T(512)S(1)}, f32[512]{0:T(512)}, u32[]{:S(2)}) copy-start(f32[512]{0:T(512)} %param.20) | copy-start | bytes 6148
  22.3 18.5 %all-to-all-start = ((s32[32,1,128]{2,1,0:T(1,128)}), s32[32,1,128]{2,1,0:T(1,128)S(1)}, u32[]{:S(2)}, u32[]{:S(2)}) async-start(s32[32,1,128]{2,1,0:T(1,128)} %spread.1), calls=%async_computation | async-start | bytes 32768 | tf_op jit(solution)/shard_map/all_to_all | solution.py:220
  30.7 2.3 %copy-start.16 = (bf16[4608,512]{1,0:T(8,128)(2,1)S(1)}, bf16[4608,512]{1,0:T(8,128)(2,1)}, u32[]{:S(2)}) copy-start(bf16[4608,512]{1,0:T(8,128)(2,1)} %copy-done.15) | copy-start | bytes 14155780
  33.1 1.6 %copy-start.18 = (bf16[512,2048]{1,0:T(8,128)(2,1)S(1)}, bf16[512,2048]{1,0:T(8,128)(2,1)}, u32[]{:S(2)}) copy-start(bf16[512,2048]{1,0:T(8,128)(2,1)} %copy-done.17) | copy-start | bytes 6291460
  34.7 1.5 %copy-start.20 = (bf16[8,49,2048]{2,1,0:T(8,128)(2,1)S(1)}, bf16[8,49,2048]{2,1,0:T(8,128)(2,1)}, u32[]{:S(2)}) copy-start(bf16[8,49,2048]{2,1,0:T(8,128)(2,1)} %copy-done.19) | copy-start | bytes 4816900

commit v3 on v2

--- a/solution.py
+++ b/solution.py
@@ -25,41 +25,55 @@
     count, cells, channels = maps.shape
     inner = w_reduce.shape[1]
     even = cells - 1
-    framed[...] = jnp.zeros(framed.shape, framed.dtype)
+    edge = jnp.zeros((SIDE, count, inner), framed.dtype)
+    framed[:, :count, :] = edge
+    framed[:, (SIDE + 1) * count :, :] = edge
     ready(0)
     for t in range(count):
         last_cell[t : t + 1, :] = maps[t, even:cells, :].astype(jnp.float32)
     x_last = last_cell[...].astype(jnp.bfloat16)
+    rows = jnp.concatenate([maps[:, 0:even, :].reshape(count * even, channels), x_last], axis=0)
     for n in range(0, inner, COLS):
         cols = slice(n, n + COLS)
-        w = w_reduce[:, cols]
-        most = jnp.dot(maps[:, 0:even, :].reshape(count * even, channels), w, preferred_element_type=jnp.float32)
-        most = jnp.maximum(most * scale_reduce[:, cols] + bias_reduce[:, cols], 0.0)
-        last = jnp.dot(x_last, w, preferred_element_type=jnp.float32)
-        last = jnp.maximum(last * scale_reduce[:, cols] + bias_reduce[:, cols], 0.0)
+        grown = jnp.dot(rows, w_reduce[:, cols], preferred_element_type=jnp.float32)
+        grown = jnp.maximum(grown * scale_reduce[:, cols] + bias_reduce[:, cols], 0.0)
         for q in range(COLS // LANES):
             block = n // LANES + q
             lanes = slice(q * LANES, (q + 1) * LANES)
             for t in range(count):
-                by_cell[block, pl.ds(t, even, stride=count), :] = most[t * even : (t + 1) * even, lanes]
-            by_cell[block, even * count :, :] = last[:, lanes]
+                by_cell[block, pl.ds(t, even, stride=count), :] = grown[t * even : (t + 1) * even, lanes]
+            by_cell[block, even * count :, :] = grown[even * count :, lanes]
     for i in range(SIDE):
         for block in range(inner // LANES):
-            framed[i + 1, count : count + SIDE * count, block * LANES : (block + 1) * LANES] = by_cell[
+            framed[i, count : count + SIDE * count, block * LANES : (block + 1) * LANES] = by_cell[
                 block, i * SIDE * count : (i + 1) * SIDE * count, :
             ].astype(jnp.bfloat16)
     ready(1)
+    row_cells = SIDE * count
     for n in range(0, inner, COLS):
         cols = slice(n, n + COLS)
-        windows = jnp.concatenate(
+        parts = []
+        for a in (1, 0, 2):
+            first, final = max(0, a - 1), min(SIDE, SIDE + a - 1)
+            windows = jnp.concatenate(
+                [
+                    framed[first:final, b * count : (b + SIDE) * count, :].reshape((final - first) * row_cells, inner)
+                    for b in range(3)
+                ],
+                axis=1,
+            )
+            parts.append(
+                jnp.dot(windows, w_spatial[a * 3 * inner : (a + 1) * 3 * inner, cols], preferred_element_type=jnp.float32)
+            )
+        middle, above, below = parts
+        conv = jnp.concatenate(
             [
-                framed[a : a + SIDE, b * count : (b + SIDE) * count, :].reshape(cells * count, inner)
-                for a in range(3)
-                for b in range(3)
+                middle[:row_cells] + below[:row_cells],
+                middle[row_cells:-row_cells] + above[:-row_cells] + below[row_cells:],
+                middle[-row_cells:] + above[-row_cells:],
             ],
-            axis=1,
+            axis=0,
         )
-        conv = jnp.dot(windows, w_spatial[:, cols], preferred_element_type=jnp.float32)
         conv = jnp.maximum(conv * scale_spatial[:, cols] + bias_spatial[:, cols], 0.0)
         for q in range(COLS // LANES):
             by_cell[n // LANES + q, :, :] = conv[:, q * LANES : (q + 1) * LANES]
@@ -85,7 +99,7 @@
     return [
         pltpu.VMEM((SEQ_DEV, channels), jnp.float32),
         pltpu.VMEM((inner // LANES, cells * SEQ_DEV, LANES), jnp.float32),
-        pltpu.VMEM((SIDE + 2, (SIDE + 2) * SEQ_DEV, inner), jnp.bfloat16),
+        pltpu.VMEM((SIDE, (SIDE + 2) * SEQ_DEV, inner), jnp.bfloat16),
         pltpu.VMEM((cells * SEQ_DEV, inner), jnp.bfloat16),
     ]
 
@@ -103,7 +117,7 @@
     own = maps.shape[0]
     loads = []
     for t in range(own):
-        slot = jnp.clip(count[0, 0] - own + t, 0, 2 * own - 1)
+        slot = lax.rem(jnp.clip(count[0, 0], 0, 2 * own) + own + t, 2 * own)
         loads.append(pltpu.make_async_copy(tiles.at[listing[0, slot]], maps.at[t], sem.at[t]))
     later = [
         pltpu.make_async_copy(w_spatial_far, w_spatial, sem.at[own]),
@@ -112,13 +126,15 @@
     later += [
         pltpu.make_async_copy(tiles.at[listing[0, t]], head_maps.at[t], sem.at[own + 2 + t]) for t in range(own)
     ]
-    for copy in loads + later:
+    for copy in loads + later[:1]:
         copy.start()
 
     def ready(stage):
         if stage == 0:
             for copy in loads:
                 copy.wait()
+            for copy in later[1:]:
+                copy.start()
         else:
             later[stage - 1].wait()
 

time: 42.2 us -> 40.5 us (0.960)
  starting transfers between devices: 10.7 us -> 9.52 us
  Pallas kernels: 13.5 us -> 13 us
    all_to_all x1, starting transfers between devices: 8.33 us -> 7.13 us  [on_device(): ahead = lax.all_to_all(spread(rank, count, devices), AXES, 0, 0, tiled=True)]
  transfers between devices with their start and end apart: 2 -> 2, of which waited for: 0 -> 0; matrix products, arithmetic and copies ran while one was open for 0% -> 0% of each run, Pallas kernels for 13% -> 12%
where the time goes in v3:
time: 40.5 us; the launch traced here: 40 us
  local copies, waits for them, and re-layouts  16.6 us (41%)
  Pallas kernels  13 us (32%)
  starting transfers between devices  9.52 us (24%)
  between operations  0.85 us (2%)
    unnamed x42, local copies, waits for them, and re-layouts  16.6 us
    pallas_call x1, Pallas kernels, encode_tail(): pl.pallas_call(tail_body, out_shape=[pltpu.VMEM((SEQ_DEV, channels), jnp....  7.22 us
    all_to_all x1, starting transfers between devices, on_device(): ahead = lax.all_to_all(spread(rank, count, devices), AXES, 0, 0, tiled=True)  7.13 us
    pallas_call x1, Pallas kernels, encode_head(): pl.pallas_call(head_body, out_shape=pltpu.VMEM((SEQ_DEV, channels), jnp.b...  4.29 us
    ppermute x1, starting transfers between devices, on_device(): arrived = lax.ppermute(tail, AXES, [(i, i + 1) for i in range(devices - 1)])  2.39 us
    pallas_call x1, Pallas kernels, pack(): pl.pallas_call(pack_body, out_shape=jax.ShapeDtypeStruct(head.shape, head...  0.85 us
  transfers between devices with their start and end apart: 2, of which 0 were waited for; matrix products, arithmetic and copies ran while one was open for 0% of the time, Pallas kernels for 12%

profile of v3, /device:TPU:0, one launch (start us, length us, event | category | flops | bytes accessed | tf_op | source)
XLA Modules:
  0.0 40.0 jit_solution(125027919143138401)
XLA Ops:
  0.7 0.0 copy-start
  0.7 1.6 %copy-done = bf16[2048,512]{1,0:T(8,128)(2,1)S(1)} copy-done((bf16[2048,512]{1,0:T(8,128)(2,1)S(1)}, bf16[2048,512]{1,0:T(8,128)(2,1)}, u32[]{:S(2)}) %copy-start) | copy-done | bytes 2097176
  2.2 0.0 copy-start.2
  2.2 0.7 %copy-done.2 = f32[2048]{0:T(1024)S(1)} copy-done((f32[2048]{0:T(1024)S(1)}, f32[2048]{0:T(1024)}, u32[]{:S(2)}) %copy-start.2) | copy-done | bytes 8216
  2.9 0.0 copy-start.4
  2.9 0.7 %copy-done.4 = f32[2048]{0:T(1024)S(1)} copy-done((f32[2048]{0:T(1024)S(1)}, f32[2048]{0:T(1024)}, u32[]{:S(2)}) %copy-start.4) | copy-done | bytes 8216
  3.6 0.0 copy-start.6
  3.6 0.7 %copy-done.6 = f32[512]{0:T(512)S(1)} copy-done((f32[512]{0:T(512)S(1)}, f32[512]{0:T(512)}, u32[]{:S(2)}) %copy-start.6) | copy-done | bytes 2072
  4.3 0.0 copy-start.8
  4.3 0.7 %copy-done.8 = f32[512]{0:T(512)S(1)} copy-done((f32[512]{0:T(512)S(1)}, f32[512]{0:T(512)}, u32[]{:S(2)}) %copy-start.8) | copy-done | bytes 2072
  5.0 0.0 copy-start.10
  5.0 0.7 %copy-done.10 = f32[512]{0:T(512)S(1)} copy-done((f32[512]{0:T(512)S(1)}, f32[512]{0:T(512)}, u32[]{:S(2)}) %copy-start.10) | copy-done | bytes 2072
  5.7 0.0 copy-start.12
  5.7 0.7 %copy-done.12 = f32[512]{0:T(512)S(1)} copy-done((f32[512]{0:T(512)S(1)}, f32[512]{0:T(512)}, u32[]{:S(2)}) %copy-start.12) | copy-done | bytes 2072
  6.4 0.0 copy-start.14
  6.4 0.7 %copy-done.14 = s32[1,18]{1,0:T(1,128)S(1)} copy-done((s32[1,18]{1,0:T(1,128)S(1)}, s32[1,18]{1,0:T(1,128)}, u32[]{:S(2)}) %copy-start.14) | copy-done | bytes 96
  7.0 7.2 %encode_tail.1 = (bf16[8,2048]{1,0:T(8,128)(2,1)S(1)}, bf16[8,49,2048]{2,1,0:T(8,128)(2,1)S(1)}, bf16[4608,512]{1,0:T(8,128)(2,1)S(1)}, bf16[512,2048]{1,0:T(8,128)(2,1)S(1)}) custom-call(s32[1,18]{1,0:T(1,128)S(1)} %copy-done.14, s32[1,1]{1,0:T(1,128)} %bitcast.10.count, bf16[18,49,2048]{2,1,0:T(8,128)(2,1)} %tiles.1, bf16[4608,512]{1,0:T(8,128)(2,1)} %bitcast.23, ...), custom_call_target="tpu_custom_call" | custom-call | flops 3493855232 | bytes 10518528 | tf_op jit(solution)/shard_map/encode_tail/pallas_call | solution.py:150
  14.2 0.0 copy-start.15
  14.3 2.1 %copy-done.15 = bf16[4608,512]{1,0:T(8,128)(2,1)} copy-done((bf16[4608,512]{1,0:T(8,128)(2,1)}, bf16[4608,512]{1,0:T(8,128)(2,1)S(1)}, u32[]{:S(2)}) %copy-start.15) | copy-done | bytes 4718616
  16.4 0.0 copy-start.17
  16.4 1.4 %copy-done.17 = bf16[512,2048]{1,0:T(8,128)(2,1)} copy-done((bf16[512,2048]{1,0:T(8,128)(2,1)}, bf16[512,2048]{1,0:T(8,128)(2,1)S(1)}, u32[]{:S(2)}) %copy-start.17) | copy-done | bytes 2097176
  17.7 0.0 copy-start.19
  17.7 1.3 %copy-done.19 = bf16[8,49,2048]{2,1,0:T(8,128)(2,1)} copy-done((bf16[8,49,2048]{2,1,0:T(8,128)(2,1)}, bf16[8,49,2048]{2,1,0:T(8,128)(2,1)S(1)}, u32[]{:S(2)}) %copy-start.19) | copy-done | bytes 1605656
  19.1 2.4 %collective-permute-start = (bf16[8,2048]{1,0:T(8,128)(2,1)S(1)}, bf16[8,2048]{1,0:T(8,128)(2,1)S(1)}, u32[]{:S(2)}, u32[]{:S(2)}) collective-permute-start(bf16[8,2048]{1,0:T(8,128)(2,1)S(1)} %get-tuple-element.9), channel_id=1, source_target_pairs={{0,1},{1,2},{2,3},{3,4},{4,5},{5,6},{6,7},{7,8},{8,9},{9,10},{10,1... | collective-permute-start | bytes 98312 | tf_op jit(solution)/shard_map/ppermute | solution.py:240
  21.5 0.0 copy-start.1
  21.5 0.0 copy-start.3
  21.5 0.0 copy-start.5
  21.5 0.0 copy-start.7
  21.5 0.0 copy-start.9
  21.5 0.0 copy-start.11
  21.5 0.0 copy-start.13
  21.6 0.6 %spread.1 = s32[32,1,128]{2,1,0:T(1,128)} custom-call(s32[1,1]{1,0:T(1,128)} %bitcast.where, s32[1,1]{1,0:T(1,128)} %bitcast.9.count), custom_call_target="tpu_custom_call" | custom-call | flops 99999997952 | bytes 100000000 | tf_op jit(solution)/shard_map/spread/pallas_call | solution.py:216
  22.2 7.1 %all-to-all-start = ((s32[32,1,128]{2,1,0:T(1,128)}), s32[32,1,128]{2,1,0:T(1,128)S(1)}, u32[]{:S(2)}, u32[]{:S(2)}) async-start(s32[32,1,128]{2,1,0:T(1,128)} %spread.1), calls=%async_computation | async-start | bytes 32768 | tf_op jit(solution)/shard_map/all_to_all | solution.py:236
  29.3 0.0 copy-done.1
  29.3 0.0 copy-done.3
  29.3 0.0 copy-done.5
  29.3 0.0 copy-done.7
  29.4 0.0 copy-done.9
  29.4 0.0 copy-done.11
  29.4 0.0 copy-done.13
  29.4 0.0 copy-start.16
  29.4 2.3 %copy-done.16 = bf16[4608,512]{1,0:T(8,128)(2,1)S(1)} copy-done((bf16[4608,512]{1,0:T(8,128)(2,1)S(1)}, bf16[4608,512]{1,0:T(8,128)(2,1)}, u32[]{:S(2)}) %copy-start.16) | copy-done | bytes 4718616
  31.7 0.0 copy-start.18
  31.7 1.6 %copy-done.18 = bf16[512,2048]{1,0:T(8,128)(2,1)S(1)} copy-done((bf16[512,2048]{1,0:T(8,128)(2,1)S(1)}, bf16[512,2048]{1,0:T(8,128)(2,1)}, u32[]{:S(2)}) %copy-start.18) | copy-done | bytes 2097176
  33.3 0.0 copy-start.20
  33.3 1.5 %copy-done.20 = bf16[8,49,2048]{2,1,0:T(8,128)(2,1)S(1)} copy-done((bf16[8,49,2048]{2,1,0:T(8,128)(2,1)S(1)}, bf16[8,49,2048]{2,1,0:T(8,128)(2,1)}, u32[]{:S(2)}) %copy-start.20) | copy-done | bytes 1605656
  34.8 4.3 %encode_head.1.head = bf16[8,2048]{1,0:T(8,128)(2,1)S(1)} custom-call(bf16[8,49,2048]{2,1,0:T(8,128)(2,1)S(1)} %copy-done.20, bf16[2048,512]{1,0:T(8,128)(2,1)S(1)} %copy-done.1, f32[1,512]{1,0:T(1,128)S(1)} %bitcast.16, f32[1,512]{1,0:T(1,128)S(1)} %bitcast.18, bf16[4608,512]{1,0:T(8,128)(2,1)S(1)} %copy-done.16, f32[1,512]{1,0:T(1,128)S(1)} %bitcast.20, ...), custom_call_target="tpu_custom_call" | custom-call | flops 3493855232 | bytes 10518528 | tf_op jit(solution)/shard_map/encode_head/pallas_call | solution.py:176
  39.1 0.0 all-to-all-done.ahead
  39.1 0.0 collective-permute-done.arrived
  39.1 0.8 %pack.1 = bf16[8,2048]{1,0:T(8,128)(2,1)} custom-call(s32[32,1,128]{2,1,0:T(1,128)S(1)} %all-to-all-done.ahead, bf16[8,2048]{1,0:T(8,128)(2,1)S(1)} %collective-permute-done.arrived, bf16[8,2048]{1,0:T(8,128)(2,1)S(1)} %encode_head.1.head), custom_call_target="tpu_custom_call" | custom-call | tf_op jit(solution)/shard_map/pack/pallas_call | solution.py:199
Async XLA Ops:
  0.7 1.6 %copy-start = (bf16[2048,512]{1,0:T(8,128)(2,1)S(1)}, bf16[2048,512]{1,0:T(8,128)(2,1)}, u32[]{:S(2)}) copy-start(bf16[2048,512]{1,0:T(8,128)(2,1)} %w_reduce.3) | copy-start | bytes 6291460
  2.2 0.7 %copy-start.2 = (f32[2048]{0:T(1024)S(1)}, f32[2048]{0:T(1024)}, u32[]{:S(2)}) copy-start(f32[2048]{0:T(1024)} %param.22) | copy-start | bytes 24580
  2.9 0.7 %copy-start.4 = (f32[2048]{0:T(1024)S(1)}, f32[2048]{0:T(1024)}, u32[]{:S(2)}) copy-start(f32[2048]{0:T(1024)} %param.23) | copy-start | bytes 24580
  3.6 0.7 %copy-start.6 = (f32[512]{0:T(512)S(1)}, f32[512]{0:T(512)}, u32[]{:S(2)}) copy-start(f32[512]{0:T(512)} %param.16) | copy-start | bytes 6148
  4.3 0.7 %copy-start.8 = (f32[512]{0:T(512)S(1)}, f32[512]{0:T(512)}, u32[]{:S(2)}) copy-start(f32[512]{0:T(512)} %param.17) | copy-start | bytes 6148
  5.0 0.7 %copy-start.10 = (f32[512]{0:T(512)S(1)}, f32[512]{0:T(512)}, u32[]{:S(2)}) copy-start(f32[512]{0:T(512)} %param.19) | copy-start | bytes 6148
  5.7 0.7 %copy-start.12 = (f32[512]{0:T(512)S(1)}, f32[512]{0:T(512)}, u32[]{:S(2)}) copy-start(f32[512]{0:T(512)} %param.20) | copy-start | bytes 6148
  6.4 0.7 %copy-start.14 = (s32[1,18]{1,0:T(1,128)S(1)}, s32[1,18]{1,0:T(1,128)}, u32[]{:S(2)}) copy-start(s32[1,18]{1,0:T(1,128)} %listing.1) | copy-start | bytes 220
  14.2 2.1 %copy-start.15 = (bf16[4608,512]{1,0:T(8,128)(2,1)}, bf16[4608,512]{1,0:T(8,128)(2,1)S(1)}, u32[]{:S(2)}) copy-start(bf16[4608,512]{1,0:T(8,128)(2,1)S(1)} %get-tuple-element.11.w_spatial) | copy-start | bytes 14155780
  16.4 1.4 %copy-start.17 = (bf16[512,2048]{1,0:T(8,128)(2,1)}, bf16[512,2048]{1,0:T(8,128)(2,1)S(1)}, u32[]{:S(2)}) copy-start(bf16[512,2048]{1,0:T(8,128)(2,1)S(1)} %get-tuple-element.12.w_expand) | copy-start | bytes 6291460
  17.7 1.3 %copy-start.19 = (bf16[8,49,2048]{2,1,0:T(8,128)(2,1)}, bf16[8,49,2048]{2,1,0:T(8,128)(2,1)S(1)}, u32[]{:S(2)}) copy-start(bf16[8,49,2048]{2,1,0:T(8,128)(2,1)S(1)} %get-tuple-element.10.maps) | copy-start | bytes 4816900
  19.1 20.1 %collective-permute-start = (bf16[8,2048]{1,0:T(8,128)(2,1)S(1)}, bf16[8,2048]{1,0:T(8,128)(2,1)S(1)}, u32[]{:S(2)}, u32[]{:S(2)}) collective-permute-start(bf16[8,2048]{1,0:T(8,128)(2,1)S(1)} %get-tuple-element.9), channel_id=1, source_target_pairs={{0,1},{1,2},{2,3},{3,4},{4,5},{5,6},{6,7},{7,8},{8,9},{9,10},{10,1... | collective-permute-start | bytes 98312 | tf_op jit(solution)/shard_map/ppermute | solution.py:240
  21.5 7.8 %copy-start.1 = (bf16[2048,512]{1,0:T(8,128)(2,1)S(1)}, bf16[2048,512]{1,0:T(8,128)(2,1)}, u32[]{:S(2)}) copy-start(bf16[2048,512]{1,0:T(8,128)(2,1)} %w_reduce.3) | copy-start | bytes 6291460
  21.5 7.8 %copy-start.3 = (f32[2048]{0:T(1024)S(1)}, f32[2048]{0:T(1024)}, u32[]{:S(2)}) copy-start(f32[2048]{0:T(1024)} %param.22) | copy-start | bytes 24580
  21.5 7.8 %copy-start.5 = (f32[2048]{0:T(1024)S(1)}, f32[2048]{0:T(1024)}, u32[]{:S(2)}) copy-start(f32[2048]{0:T(1024)} %param.23) | copy-start | bytes 24580
  21.5 7.8 %copy-start.7 = (f32[512]{0:T(512)S(1)}, f32[512]{0:T(512)}, u32[]{:S(2)}) copy-start(f32[512]{0:T(512)} %param.16) | copy-start | bytes 6148
  21.5 7.8 %copy-start.9 = (f32[512]{0:T(512)S(1)}, f32[512]{0:T(512)}, u32[]{:S(2)}) copy-start(f32[512]{0:T(512)} %param.17) | copy-start | bytes 6148
  21.5 7.8 %copy-start.11 = (f32[512]{0:T(512)S(1)}, f32[512]{0:T(512)}, u32[]{:S(2)}) copy-start(f32[512]{0:T(512)} %param.19) | copy-start | bytes 6148
  21.5 7.8 %copy-start.13 = (f32[512]{0:T(512)S(1)}, f32[512]{0:T(512)}, u32[]{:S(2)}) copy-start(f32[512]{0:T(512)} %param.20) | copy-start | bytes 6148
  22.2 16.9 %all-to-all-start = ((s32[32,1,128]{2,1,0:T(1,128)}), s32[32,1,128]{2,1,0:T(1,128)S(1)}, u32[]{:S(2)}, u32[]{:S(2)}) async-start(s32[32,1,128]{2,1,0:T(1,128)} %spread.1), calls=%async_computation | async-start | bytes 32768 | tf_op jit(solution)/shard_map/all_to_all | solution.py:236
  29.4 2.3 %copy-start.16 = (bf16[4608,512]{1,0:T(8,128)(2,1)S(1)}, bf16[4608,512]{1,0:T(8,128)(2,1)}, u32[]{:S(2)}) copy-start(bf16[4608,512]{1,0:T(8,128)(2,1)} %copy-done.15) | copy-start | bytes 14155780
  31.7 1.6 %copy-start.18 = (bf16[512,2048]{1,0:T(8,128)(2,1)S(1)}, bf16[512,2048]{1,0:T(8,128)(2,1)}, u32[]{:S(2)}) copy-start(bf16[512,2048]{1,0:T(8,128)(2,1)} %copy-done.17) | copy-start | bytes 6291460
  33.3 1.5 %copy-start.20 = (bf16[8,49,2048]{2,1,0:T(8,128)(2,1)S(1)}, bf16[8,49,2048]{2,1,0:T(8,128)(2,1)}, u32[]{:S(2)}) copy-start(bf16[8,49,2048]{2,1,0:T(8,128)(2,1)} %copy-done.19) | copy-start | bytes 4816900

commit v4 on v3

--- a/solution.py
+++ b/solution.py
@@ -115,16 +115,22 @@
 def tail_body(listing, count, tiles, w_spatial_far, w_expand_far, w_reduce, s1, b1, s2, b2, s3, b3, tail, head_maps, w_spatial, w_expand, maps, *rest):
     *work, sem = rest
     own = maps.shape[0]
+    row = lax.broadcasted_iota(jnp.int32, (2 * own, listing.shape[1]), 0)
+    lane = lax.broadcasted_iota(jnp.int32, (2 * own, listing.shape[1]), 1)
+    amount = jnp.clip(count[:, : listing.shape[1]], 0, 2 * own)
+    place = amount + own + row
+    place = jnp.where(row < own, jnp.where(place >= 2 * own, place - 2 * own, place), row - own)
+    place = jnp.where(place >= 2 * own, place - 2 * own, place)
+    chosen = jnp.sum(jnp.where(lane == place, listing[...], 0), axis=1, keepdims=True)
     loads = []
     for t in range(own):
-        slot = lax.rem(jnp.clip(count[0, 0], 0, 2 * own) + own + t, 2 * own)
-        loads.append(pltpu.make_async_copy(tiles.at[listing[0, slot]], maps.at[t], sem.at[t]))
+        loads.append(pltpu.make_async_copy(tiles.at[chosen[t, 0]], maps.at[t], sem.at[t]))
     later = [
         pltpu.make_async_copy(w_spatial_far, w_spatial, sem.at[own]),
         pltpu.make_async_copy(w_expand_far, w_expand, sem.at[own + 1]),
     ]
     later += [
-        pltpu.make_async_copy(tiles.at[listing[0, t]], head_maps.at[t], sem.at[own + 2 + t]) for t in range(own)
+        pltpu.make_async_copy(tiles.at[chosen[own + t, 0]], head_maps.at[t], sem.at[own + 2 + t]) for t in range(own)
     ]
     for copy in loads + later[:1]:
         copy.start()
@@ -155,7 +161,7 @@
             pltpu.VMEM(w_spatial.shape, w_spatial.dtype),
             pltpu.VMEM(w_expand.shape, w_expand.dtype),
         ],
-        in_specs=[SCALAR] * 2 + [FAR] * 3 + [NEAR] * 7,
+        in_specs=[NEAR] * 2 + [FAR] * 3 + [NEAR] * 7,
         out_specs=[NEAR] * 4,
         scratch_shapes=[pltpu.VMEM(maps, tiles.dtype)]
         + scratch(cells, channels, inner)
@@ -163,7 +169,7 @@
         cost_estimate=cost(cells, channels, inner),
         compiler_params=pltpu.CompilerParams(vmem_limit_bytes=40 << 20),
         name="encode_tail",
-    )(listing, count, *(pltpu.with_memory_space_constraint(v, pltpu.HBM) for v in (tiles, w_spatial, w_expand)), w_reduce, s1, b1, s2, b2, s3, b3)
+    )(held(listing), count, *(pltpu.with_memory_space_constraint(v, pltpu.HBM) for v in (tiles, w_spatial, w_expand)), w_reduce, s1, b1, s2, b2, s3, b3)
 
 
 def head_body(maps, w_reduce, s1, b1, w_spatial, s2, b2, w_expand, s3, b3, head, *work):
@@ -207,7 +213,8 @@
     )(held(ahead), held(arrived), held(head))
 
 
-def spread_body(where, count, out):
+def spread_body(where, count, out, again):
+    again[...] = jnp.full(again.shape, count[0, 0])
     place = lax.broadcasted_iota(jnp.int32, out.shape, 0)
     out[...] = jnp.where(place > where[0, 0], count[0, 0] - SEQ_DEV, 0)
 
@@ -215,9 +222,9 @@
 def spread(where, count, devices):
     return pl.pallas_call(
         spread_body,
-        out_shape=jax.ShapeDtypeStruct((devices, 1, LANES), jnp.int32),
+        out_shape=[jax.ShapeDtypeStruct((devices, 1, LANES), jnp.int32), pltpu.VMEM((1, LANES), jnp.int32)],
         in_specs=[SCALAR] * 2,
-        out_specs=NEAR,
+        out_specs=[NEAR] * 2,
         cost_estimate=pl.CostEstimate(flops=10**11, bytes_accessed=10**8, transcendentals=0),
         compiler_params=pltpu.CompilerParams(vmem_limit_bytes=1 << 20),
         name="spread",
@@ -233,7 +240,8 @@
     w_reduce, s1, b1, s2, b2, s3, b3 = (
         held(v.reshape(-1, v.shape[-1])) for v in (w_reduce, s1, b1, s2, b2, s3, b3)
     )
-    ahead = lax.all_to_all(spread(rank, count, devices), AXES, 0, 0, tiled=True)
+    adds, count = spread(rank, count, devices)
+    ahead = lax.all_to_all(adds, AXES, 0, 0, tiled=True)
     tail, maps, w_spatial, w_expand = encode_tail(
         tissue_index, count, tiles, w_reduce, s1, b1, w_spatial, s2, b2, w_expand, s3, b3
     )

time: 40.5 us -> 24.2 us (0.60)
  the two profiles are of different devices: /device:TPU:0 before, /device:TPU:4 now
where the time goes in v4:
time: 24.2 us; the launch traced here: 24 us
  Pallas kernels  12.5 us (52%)
  starting transfers between devices  8.12 us (34%)
  waiting for transfers between devices  2.48 us (10%)
  between operations  0.82 us (3%)
    pallas_call x1, Pallas kernels, encode_tail(): pl.pallas_call(tail_body, out_shape=[pltpu.VMEM((SEQ_DEV, channels), jnp....  6.73 us
    all_to_all x1, starting transfers between devices, on_device(): ahead = lax.all_to_all(adds, AXES, 0, 0, tiled=True)  6.1 us
    pallas_call x1, Pallas kernels, encode_head(): pl.pallas_call(head_body, out_shape=pltpu.VMEM((SEQ_DEV, channels), jnp.b...  4.31 us
    ppermute x1, waiting for transfers between devices, on_device(): arrived = lax.ppermute(tail, AXES, [(i, i + 1) for i in range(devices - 1)])  2.47 us
    ppermute x1, starting transfers between devices, on_device(): arrived = lax.ppermute(tail, AXES, [(i, i + 1) for i in range(devices - 1)])  2.02 us
    pallas_call x1, Pallas kernels, pack(): pl.pallas_call(pack_body, out_shape=jax.ShapeDtypeStruct(head.shape, head...  0.85 us
    pallas_call x1, Pallas kernels, spread(): pl.pallas_call(spread_body, out_shape=[jax.ShapeDtypeStruct((devices, 1,...  0.62 us
  transfers between devices with their start and end apart: 2, of which 1 were waited for; matrix products, arithmetic and copies ran while one was open for 0% of the time, Pallas kernels for 46%

profile of v4, /device:TPU:4, one launch (start us, length us, event | category | flops | bytes accessed | tf_op | source)
XLA Modules:
  0.0 24.0 jit_solution(16429885497112474630)
XLA Ops:
  0.7 0.0 copy-start
  0.7 0.0 copy-start.1
  0.7 0.0 copy-start.2
  0.7 0.0 copy-start.3
  0.7 0.0 copy-start.4
  0.7 0.0 copy-start.5
  0.7 0.0 copy-start.6
  0.7 0.0 copy-start.7
  0.7 0.6 %spread.1 = (s32[32,1,128]{2,1,0:T(1,128)}, s32[1,128]{1,0:T(1,128)S(1)}) custom-call(s32[1,1]{1,0:T(1,128)} %bitcast.where, s32[1,1]{1,0:T(1,128)} %bitcast.9.count), custom_call_target="tpu_custom_call" | custom-call | flops 99999997952 | bytes 100000000 | tf_op jit(solution)/shard_map/spread/pallas_call | solution.py:223
  1.4 6.1 %all-to-all-start = ((s32[32,1,128]{2,1,0:T(1,128)}), s32[32,1,128]{2,1,0:T(1,128)S(1)}, u32[]{:S(2)}, u32[]{:S(2)}) async-start(s32[32,1,128]{2,1,0:T(1,128)} %get-tuple-element.11), calls=%async_computation | async-start | bytes 32768 | tf_op jit(solution)/shard_map/all_to_all | solution.py:244
  7.5 0.0 copy-done
  7.5 0.0 copy-done.1
  7.5 0.0 copy-done.2
  7.5 0.0 copy-done.3
  7.5 0.0 copy-done.4
  7.5 0.0 copy-done.5
  7.5 0.0 copy-done.6
  7.5 0.0 copy-done.7
  7.5 6.7 %encode_tail.1 = (bf16[8,2048]{1,0:T(8,128)(2,1)S(1)}, bf16[8,49,2048]{2,1,0:T(8,128)(2,1)S(1)}, bf16[4608,512]{1,0:T(8,128)(2,1)S(1)}, bf16[512,2048]{1,0:T(8,128)(2,1)S(1)}) custom-call(s32[1,18]{1,0:T(1,128)S(1)} %copy-done.7, s32[1,128]{1,0:T(1,128)S(1)} %get-tuple-element.12.count, bf16[18,49,2048]{2,1,0:T(8,128)(2,1)} %tiles.1, ...), custom_call_target="tpu_custom_call" | custom-call | flops 3493855232 | bytes 10518528 | tf_op jit(solution)/shard_map/encode_tail/pallas_call | solution.py:156
  14.3 2.0 %collective-permute-start = (bf16[8,2048]{1,0:T(8,128)(2,1)S(1)}, bf16[8,2048]{1,0:T(8,128)(2,1)S(1)}, u32[]{:S(2)}, u32[]{:S(2)}) collective-permute-start(bf16[8,2048]{1,0:T(8,128)(2,1)S(1)} %get-tuple-element.13), channel_id=1, source_target_pairs={{0,1},{1,2},{2,3},{3,4},{4,5},{5,6},{6,7},{7,8},{8,9},{9,10},{10,1... | collective-permute-start | bytes 98312 | tf_op jit(solution)/shard_map/ppermute | solution.py:248
  16.3 4.3 %encode_head.1.head = bf16[8,2048]{1,0:T(8,128)(2,1)S(1)} custom-call(bf16[8,49,2048]{2,1,0:T(8,128)(2,1)S(1)} %get-tuple-element.14.maps, bf16[2048,512]{1,0:T(8,128)(2,1)S(1)} %copy-done, f32[1,512]{1,0:T(1,128)S(1)} %bitcast.15, f32[1,512]{1,0:T(1,128)S(1)} %bitcast.17, bf16[4608,512]{1,0:T(8,128)(2,1)S(1)} %get-tuple-element.15.w_spatial, ...), custom_call_target="tpu_custom_call" | custom-call | flops 3493855232 | bytes 10518528 | tf_op jit(solution)/shard_map/encode_head/pallas_call | solution.py:182
  20.6 0.0 all-to-all-done.ahead
  20.6 2.5 %collective-permute-done.arrived = bf16[8,2048]{1,0:T(8,128)(2,1)S(1)} collective-permute-done((bf16[8,2048]{1,0:T(8,128)(2,1)S(1)}, bf16[8,2048]{1,0:T(8,128)(2,1)S(1)}, u32[]{:S(2)}, u32[]{:S(2)}) %collective-permute-start) | collective-permute-done | bytes 32800 | tf_op jit(solution)/shard_map/ppermute | solution.py:248
  23.1 0.8 %pack.1 = bf16[8,2048]{1,0:T(8,128)(2,1)} custom-call(s32[32,1,128]{2,1,0:T(1,128)S(1)} %all-to-all-done.ahead, bf16[8,2048]{1,0:T(8,128)(2,1)S(1)} %collective-permute-done.arrived, bf16[8,2048]{1,0:T(8,128)(2,1)S(1)} %encode_head.1.head), custom_call_target="tpu_custom_call" | custom-call | tf_op jit(solution)/shard_map/pack/pallas_call | solution.py:205
Async XLA Ops:
  0.7 6.8 %copy-start = (bf16[2048,512]{1,0:T(8,128)(2,1)S(1)}, bf16[2048,512]{1,0:T(8,128)(2,1)}, u32[]{:S(2)}) copy-start(bf16[2048,512]{1,0:T(8,128)(2,1)} %w_reduce.3) | copy-start | bytes 6291460
  0.7 6.8 %copy-start.1 = (f32[2048]{0:T(1024)S(1)}, f32[2048]{0:T(1024)}, u32[]{:S(2)}) copy-start(f32[2048]{0:T(1024)} %param.22) | copy-start | bytes 24580
  0.7 6.8 %copy-start.2 = (f32[2048]{0:T(1024)S(1)}, f32[2048]{0:T(1024)}, u32[]{:S(2)}) copy-start(f32[2048]{0:T(1024)} %param.23) | copy-start | bytes 24580
  0.7 6.8 %copy-start.3 = (f32[512]{0:T(512)S(1)}, f32[512]{0:T(512)}, u32[]{:S(2)}) copy-start(f32[512]{0:T(512)} %param.16) | copy-start | bytes 6148
  0.7 6.8 %copy-start.4 = (f32[512]{0:T(512)S(1)}, f32[512]{0:T(512)}, u32[]{:S(2)}) copy-start(f32[512]{0:T(512)} %param.17) | copy-start | bytes 6148
  0.7 6.8 %copy-start.5 = (f32[512]{0:T(512)S(1)}, f32[512]{0:T(512)}, u32[]{:S(2)}) copy-start(f32[512]{0:T(512)} %param.19) | copy-start | bytes 6148
  0.7 6.8 %copy-start.6 = (f32[512]{0:T(512)S(1)}, f32[512]{0:T(512)}, u32[]{:S(2)}) copy-start(f32[512]{0:T(512)} %param.20) | copy-start | bytes 6148
  0.7 6.8 %copy-start.7 = (s32[1,18]{1,0:T(1,128)S(1)}, s32[1,18]{1,0:T(1,128)}, u32[]{:S(2)}) copy-start(s32[1,18]{1,0:T(1,128)} %listing.1) | copy-start | bytes 220
  1.4 19.3 %all-to-all-start = ((s32[32,1,128]{2,1,0:T(1,128)}), s32[32,1,128]{2,1,0:T(1,128)S(1)}, u32[]{:S(2)}, u32[]{:S(2)}) async-start(s32[32,1,128]{2,1,0:T(1,128)} %get-tuple-element.11), calls=%async_computation | async-start | bytes 32768 | tf_op jit(solution)/shard_map/all_to_all | solution.py:244
  14.3 8.8 %collective-permute-start = (bf16[8,2048]{1,0:T(8,128)(2,1)S(1)}, bf16[8,2048]{1,0:T(8,128)(2,1)S(1)}, u32[]{:S(2)}, u32[]{:S(2)}) collective-permute-start(bf16[8,2048]{1,0:T(8,128)(2,1)S(1)} %get-tuple-element.13), channel_id=1, source_target_pairs={{0,1},{1,2},{2,3},{3,4},{4,5},{5,6},{6,7},{7,8},{8,9},{9,10},{10,1... | collective-permute-start | bytes 98312 | tf_op jit(solution)/shard_map/ppermute | solution.py:248

commit v5 on v4

--- a/solution.py
+++ b/solution.py
@@ -9,6 +9,7 @@
 SIDE = 7
 SEQ_DEV = 8
 LANES = 128
+SUBLANES = 8
 COLS = 256
 AXES = ("grp", "ext")
 SCALAR = pl.BlockSpec(memory_space=pltpu.SMEM)
@@ -20,7 +21,7 @@
     return pltpu.with_memory_space_constraint(value, pltpu.VMEM)
 
 
-def encode(maps, weights, out, last_cell, by_cell, framed, spatial, ready=lambda stage: None):
+def encode(maps, weights, out, last_cell, by_cell, framed, spatial, partial, ready=lambda stage: None):
     w_reduce, scale_reduce, bias_reduce, w_spatial, scale_spatial, bias_spatial, w_expand, scale_expand, bias_expand = weights
     count, cells, channels = maps.shape
     inner = w_reduce.shape[1]
@@ -91,8 +92,17 @@
         grown = grown * scale_expand[:, cols] + bias_expand[:, cols]
         most = grown[: even * count].reshape(count, even, COLS) + maps[:, 0:even, cols].astype(jnp.float32)
         last = grown[even * count :] + last_cell[:, cols]
-        total = jnp.sum(jnp.maximum(most, 0.0), axis=1) + jnp.maximum(last, 0.0)
-        out[:, cols] = (total / cells).astype(out.dtype)
+        most = jnp.maximum(most, 0.0).reshape(count, even // SUBLANES, SUBLANES, COLS)
+        part = jnp.sum(most, axis=1).reshape(count * SUBLANES, COLS)
+        last = jnp.maximum(last, 0.0)
+        for q in range(COLS // LANES):
+            block = n // LANES + q
+            lanes = slice(q * LANES, (q + 1) * LANES)
+            partial[block, :, :] = part[:, lanes]
+            total = last[:, lanes]
+            for sub in range(SUBLANES):
+                total = total + partial[block, pl.ds(sub, count, stride=SUBLANES), :]
+            out[:, block * LANES : (block + 1) * LANES] = (total / cells).astype(out.dtype)
 
 
 def scratch(cells, channels, inner):
@@ -101,6 +111,7 @@
         pltpu.VMEM((inner // LANES, cells * SEQ_DEV, LANES), jnp.float32),
         pltpu.VMEM((SIDE, (SIDE + 2) * SEQ_DEV, inner), jnp.bfloat16),
         pltpu.VMEM((cells * SEQ_DEV, inner), jnp.bfloat16),
+        pltpu.VMEM((channels // LANES, SEQ_DEV * SUBLANES, LANES), jnp.float32),
     ]
 
 
@@ -139,10 +150,11 @@
         if stage == 0:
             for copy in loads:
                 copy.wait()
+        else:
+            later[stage - 1].wait()
+        if stage == 1:
             for copy in later[1:]:
                 copy.start()
-        else:
-            later[stage - 1].wait()
 
     encode(maps, (w_reduce, s1, b1, w_spatial, s2, b2, w_expand, s3, b3), tail, *work, ready=ready)
     for copy in later[2:]:

time: 24.2 us -> 24.1 us (level)
  no operation moved by 1% of the time
where the time goes in v5:
time: 24.1 us; the launch traced here: 23.9 us
  Pallas kernels  12.4 us (51%)
  starting transfers between devices  8.13 us (34%)
  waiting for transfers between devices  2.54 us (11%)
  between operations  0.82 us (3%)
    pallas_call x1, Pallas kernels, encode_tail(): pl.pallas_call(tail_body, out_shape=[pltpu.VMEM((SEQ_DEV, channels), jnp....  6.65 us
    all_to_all x1, starting transfers between devices, on_device(): ahead = lax.all_to_all(adds, AXES, 0, 0, tiled=True)  6.1 us
    pallas_call x1, Pallas kernels, encode_head(): pl.pallas_call(head_body, out_shape=pltpu.VMEM((SEQ_DEV, channels), jnp.b...  4.24 us
    ppermute x1, waiting for transfers between devices, on_device(): arrived = lax.ppermute(tail, AXES, [(i, i + 1) for i in range(devices - 1)])  2.53 us
    ppermute x1, starting transfers between devices, on_device(): arrived = lax.ppermute(tail, AXES, [(i, i + 1) for i in range(devices - 1)])  2.03 us
    pallas_call x1, Pallas kernels, pack(): pl.pallas_call(pack_body, out_shape=jax.ShapeDtypeStruct(head.shape, head...  0.85 us
    pallas_call x1, Pallas kernels, spread(): pl.pallas_call(spread_body, out_shape=[jax.ShapeDtypeStruct((devices, 1,...  0.62 us
  transfers between devices with their start and end apart: 2, of which 1 were waited for; matrix products, arithmetic and copies ran while one was open for 0% of the time, Pallas kernels for 46%

profile of v5, /device:TPU:4, one launch (start us, length us, event | category | flops | bytes accessed | tf_op | source)
XLA Modules:
  0.0 23.9 jit_solution(17093245006063830324)
XLA Ops:
  0.7 0.0 copy-start
  0.7 0.0 copy-start.1
  0.7 0.0 copy-start.2
  0.7 0.0 copy-start.3
  0.7 0.0 copy-start.4
  0.7 0.0 copy-start.5
  0.7 0.0 copy-start.6
  0.7 0.0 copy-start.7
  0.7 0.6 %spread.1 = (s32[32,1,128]{2,1,0:T(1,128)}, s32[1,128]{1,0:T(1,128)S(1)}) custom-call(s32[1,1]{1,0:T(1,128)} %bitcast.where, s32[1,1]{1,0:T(1,128)} %bitcast.9.count), custom_call_target="tpu_custom_call" | custom-call | flops 99999997952 | bytes 100000000 | tf_op jit(solution)/shard_map/spread/pallas_call | solution.py:235
  1.4 6.1 %all-to-all-start = ((s32[32,1,128]{2,1,0:T(1,128)}), s32[32,1,128]{2,1,0:T(1,128)S(1)}, u32[]{:S(2)}, u32[]{:S(2)}) async-start(s32[32,1,128]{2,1,0:T(1,128)} %get-tuple-element.11), calls=%async_computation | async-start | bytes 32768 | tf_op jit(solution)/shard_map/all_to_all | solution.py:256
  7.5 0.0 copy-done
  7.5 0.0 copy-done.1
  7.5 0.0 copy-done.2
  7.5 0.0 copy-done.3
  7.5 0.0 copy-done.4
  7.5 0.0 copy-done.5
  7.5 0.0 copy-done.6
  7.5 0.0 copy-done.7
  7.5 6.6 %encode_tail.1 = (bf16[8,2048]{1,0:T(8,128)(2,1)S(1)}, bf16[8,49,2048]{2,1,0:T(8,128)(2,1)S(1)}, bf16[4608,512]{1,0:T(8,128)(2,1)S(1)}, bf16[512,2048]{1,0:T(8,128)(2,1)S(1)}) custom-call(s32[1,18]{1,0:T(1,128)S(1)} %copy-done.7, s32[1,128]{1,0:T(1,128)S(1)} %get-tuple-element.12.count, bf16[18,49,2048]{2,1,0:T(8,128)(2,1)} %tiles.1, ...), custom_call_target="tpu_custom_call" | custom-call | flops 3493855232 | bytes 10518528 | tf_op jit(solution)/shard_map/encode_tail/pallas_call | solution.py:168
  14.2 2.0 %collective-permute-start = (bf16[8,2048]{1,0:T(8,128)(2,1)S(1)}, bf16[8,2048]{1,0:T(8,128)(2,1)S(1)}, u32[]{:S(2)}, u32[]{:S(2)}) collective-permute-start(bf16[8,2048]{1,0:T(8,128)(2,1)S(1)} %get-tuple-element.13), channel_id=1, source_target_pairs={{0,1},{1,2},{2,3},{3,4},{4,5},{5,6},{6,7},{7,8},{8,9},{9,10},{10,1... | collective-permute-start | bytes 98312 | tf_op jit(solution)/shard_map/ppermute | solution.py:260
  16.2 4.2 %encode_head.1.head = bf16[8,2048]{1,0:T(8,128)(2,1)S(1)} custom-call(bf16[8,49,2048]{2,1,0:T(8,128)(2,1)S(1)} %get-tuple-element.14.maps, bf16[2048,512]{1,0:T(8,128)(2,1)S(1)} %copy-done, f32[1,512]{1,0:T(1,128)S(1)} %bitcast.15, f32[1,512]{1,0:T(1,128)S(1)} %bitcast.17, bf16[4608,512]{1,0:T(8,128)(2,1)S(1)} %get-tuple-element.15.w_spatial, ...), custom_call_target="tpu_custom_call" | custom-call | flops 3493855232 | bytes 10518528 | tf_op jit(solution)/shard_map/encode_head/pallas_call | solution.py:194
  20.5 0.0 all-to-all-done.ahead
  20.5 2.5 %collective-permute-done.arrived = bf16[8,2048]{1,0:T(8,128)(2,1)S(1)} collective-permute-done((bf16[8,2048]{1,0:T(8,128)(2,1)S(1)}, bf16[8,2048]{1,0:T(8,128)(2,1)S(1)}, u32[]{:S(2)}, u32[]{:S(2)}) %collective-permute-start) | collective-permute-done | bytes 32800 | tf_op jit(solution)/shard_map/ppermute | solution.py:260
  23.0 0.8 %pack.1 = bf16[8,2048]{1,0:T(8,128)(2,1)} custom-call(s32[32,1,128]{2,1,0:T(1,128)S(1)} %all-to-all-done.ahead, bf16[8,2048]{1,0:T(8,128)(2,1)S(1)} %collective-permute-done.arrived, bf16[8,2048]{1,0:T(8,128)(2,1)S(1)} %encode_head.1.head), custom_call_target="tpu_custom_call" | custom-call | tf_op jit(solution)/shard_map/pack/pallas_call | solution.py:217
Async XLA Ops:
  0.7 6.8 %copy-start = (bf16[2048,512]{1,0:T(8,128)(2,1)S(1)}, bf16[2048,512]{1,0:T(8,128)(2,1)}, u32[]{:S(2)}) copy-start(bf16[2048,512]{1,0:T(8,128)(2,1)} %w_reduce.3) | copy-start | bytes 6291460
  0.7 6.8 %copy-start.1 = (f32[2048]{0:T(1024)S(1)}, f32[2048]{0:T(1024)}, u32[]{:S(2)}) copy-start(f32[2048]{0:T(1024)} %param.22) | copy-start | bytes 24580
  0.7 6.8 %copy-start.2 = (f32[2048]{0:T(1024)S(1)}, f32[2048]{0:T(1024)}, u32[]{:S(2)}) copy-start(f32[2048]{0:T(1024)} %param.23) | copy-start | bytes 24580
  0.7 6.8 %copy-start.3 = (f32[512]{0:T(512)S(1)}, f32[512]{0:T(512)}, u32[]{:S(2)}) copy-start(f32[512]{0:T(512)} %param.16) | copy-start | bytes 6148
  0.7 6.8 %copy-start.4 = (f32[512]{0:T(512)S(1)}, f32[512]{0:T(512)}, u32[]{:S(2)}) copy-start(f32[512]{0:T(512)} %param.17) | copy-start | bytes 6148
  0.7 6.8 %copy-start.5 = (f32[512]{0:T(512)S(1)}, f32[512]{0:T(512)}, u32[]{:S(2)}) copy-start(f32[512]{0:T(512)} %param.19) | copy-start | bytes 6148
  0.7 6.8 %copy-start.6 = (f32[512]{0:T(512)S(1)}, f32[512]{0:T(512)}, u32[]{:S(2)}) copy-start(f32[512]{0:T(512)} %param.20) | copy-start | bytes 6148
  0.7 6.8 %copy-start.7 = (s32[1,18]{1,0:T(1,128)S(1)}, s32[1,18]{1,0:T(1,128)}, u32[]{:S(2)}) copy-start(s32[1,18]{1,0:T(1,128)} %listing.1) | copy-start | bytes 220
  1.4 19.1 %all-to-all-start = ((s32[32,1,128]{2,1,0:T(1,128)}), s32[32,1,128]{2,1,0:T(1,128)S(1)}, u32[]{:S(2)}, u32[]{:S(2)}) async-start(s32[32,1,128]{2,1,0:T(1,128)} %get-tuple-element.11), calls=%async_computation | async-start | bytes 32768 | tf_op jit(solution)/shard_map/all_to_all | solution.py:256
  14.2 8.8 %collective-permute-start = (bf16[8,2048]{1,0:T(8,128)(2,1)S(1)}, bf16[8,2048]{1,0:T(8,128)(2,1)S(1)}, u32[]{:S(2)}, u32[]{:S(2)}) collective-permute-start(bf16[8,2048]{1,0:T(8,128)(2,1)S(1)} %get-tuple-element.13), channel_id=1, source_target_pairs={{0,1},{1,2},{2,3},{3,4},{4,5},{5,6},{6,7},{7,8},{8,9},{9,10},{10,1... | collective-permute-start | bytes 98312 | tf_op jit(solution)/shard_map/ppermute | solution.py:260
